TPU v7x, 256 devices: a whole 4x4x8 slice. The times are simulated.
256 devices in a mesh: tm: 32 (over x_hi, z, core), tile: 8 (over y, x_lo).
Axes of the slice: x: 4 (x_hi: 2, x_lo: 2; x = x_hi * 2 + x_lo), y: 4, z: 8, core: 2. Of those that a mesh axis runs over, the one named last changes fastest.
Arguments:
- latent: bfloat16 [32, 16, 160, 384], P('tm', 'tile'), may hold values from -6 to 6
- gain: float32 [384], replicated, may hold values from 0.1 to 1.9
- conv_weight: bfloat16 [3, 3, 3, 384, 384], replicated, may hold values from -0.0625 to 0.0625
- conv_bias: float32 [384], replicated, may hold values from -3 to 3
- time_weight: bfloat16 [3, 384, 768], replicated, may hold values from -0.1875 to 0.1875
- time_bias: float32 [768], replicated, may hold values from -3 to 3
- up_weight: bfloat16 [3, 3, 384, 192], replicated, may hold values from -0.109375 to 0.109375
- up_bias: float32 [192], replicated, may hold values from -3 to 3
Outputs:
- decoded: bfloat16 [64, 32, 320, 192], P('tm', 'tile')
All inputs are finite; a program needn't handle non-finite values.
Results may differ from a plain program's by a relative error of at most 0.0057.
Values may be sent and summed in bfloat16 or wider, within the bound.
A program may use at most 64 MiB of HBM per device.

v0:
```python
import jax
import jax.numpy as jnp
from jax import lax
from jax.sharding import PartitionSpec as P


def shifted(block, axis, distance):
    devices = range(lax.axis_size(axis))
    route = [(i - distance, i) for i in devices if i - distance in devices]
    return lax.ppermute(block, axis, route)


def padded_2(array, sides, width):
    for axis, dim in sides:
        count, length = (lax.axis_size(axis), array.shape[dim])
        up = [(i, (i + 1) % count) for i in range(count - 1)]
        down = [(j, i) for i, j in up]
        last = lax.slice_in_dim(array, length - width, length, axis=dim)
        leading = lax.slice_in_dim(array, 0, width, axis=dim)
        before = lax.ppermute(last, axis, up)
        after = lax.ppermute(leading, axis, down)
        array = jnp.concatenate([before, array, after], axis=dim)
    return array


def activate(field, gain):
    values = field.astype(jnp.float32)
    meansq = jnp.mean(values * values, axis=-1, keepdims=True)
    scaled = values * lax.rsqrt(meansq + 1e-06) * gain
    return (scaled * jax.nn.sigmoid(scaled)).astype(jnp.bfloat16)


def history(field):
    nearer = shifted(field, "tm", 1)
    farther = shifted(field, "tm", 2)
    return jnp.concatenate([farther, nearer, field], axis=0)


def causal_conv(stacked, conv_weight):
    rows_out = stacked.shape[1] - 2
    cols = stacked.shape[2]
    chans = stacked.shape[3]
    outs_n = conv_weight.shape[4]
    padded = jnp.pad(stacked, ((0, 0), (0, 0), (1, 1), (0, 0)))
    total = jnp.zeros((rows_out * cols, outs_n), jnp.float32)
    for step_t in range(3):
        for step_h in range(3):
            slab = padded[step_t, step_h : step_h + rows_out]
            wide = jnp.concatenate(
                [slab[:, shift_w : shift_w + cols] for shift_w in range(3)], axis=-1
            )
            total = total + jnp.dot(
                wide.reshape(-1, 3 * chans),
                conv_weight[step_t, step_h].reshape(3 * chans, outs_n),
                preferred_element_type=jnp.float32,
            )
    return total.reshape(rows_out, cols, outs_n)


def time_mix(stacked, time_weight, time_bias):
    rows_n, cols, chans = (stacked.shape[1], stacked.shape[2], stacked.shape[3])
    flat = stacked.reshape(3, rows_n * cols, chans)
    halves = []
    for half in range(2):
        total = time_bias[half * chans : (half + 1) * chans] + jnp.zeros(
            (rows_n * cols, chans), jnp.float32
        )
        for step_t in range(3):
            total = total + jnp.dot(
                flat[step_t],
                time_weight[step_t, :, half * chans : (half + 1) * chans],
                preferred_element_type=jnp.float32,
            )
        halves.append(total.reshape(rows_n, cols, chans))
    return jnp.stack(halves, axis=0)


def upsample_conv(edged, up_weight, up_bias):
    rows_n = edged.shape[1] - 2
    cols2 = 2 * edged.shape[2]
    chans = edged.shape[3]
    outs_n = up_weight.shape[3]
    upsampled = jnp.repeat(jnp.repeat(edged, 2, axis=1), 2, axis=2)[:, 1 : 2 * rows_n + 3]
    padded = jnp.pad(upsampled, ((0, 0), (0, 0), (1, 1), (0, 0)))
    total = jnp.zeros((2 * 2 * rows_n * cols2, outs_n), jnp.float32)
    for step_h in range(3):
        slab = padded[:, step_h : step_h + 2 * rows_n]
        wide = jnp.concatenate(
            [slab[:, :, shift_w : shift_w + cols2] for shift_w in range(3)], axis=-1
        )
        total = total + jnp.dot(
            wide.reshape(-1, 3 * chans),
            up_weight[step_h].reshape(3 * chans, outs_n),
            preferred_element_type=jnp.float32,
        )
    return (total + up_bias).astype(jnp.bfloat16).reshape(2, 2 * rows_n, cols2, outs_n)


def local(latent, gain, conv_weight, conv_bias, time_weight, time_bias, up_weight, up_bias):
    stacked = history(activate(latent, gain))
    stacked = padded_2(stacked, (("tile", 1),), 1)
    inner = causal_conv(stacked, conv_weight)
    block = (inner + conv_bias + latent[0].astype(jnp.float32)).astype(jnp.bfloat16)
    frames = time_mix(history(block[None]), time_weight, time_bias).astype(jnp.bfloat16)
    edged = padded_2(frames, (("tile", 1),), 1)
    return upsample_conv(edged, up_weight, up_bias)


def solution(mesh):
    placed = (P("tm", "tile", None, None), P(), P(), P(), P(), P(), P(), P())
    return jax.shard_map(
        local, mesh=mesh, in_specs=placed, out_specs=P("tm", "tile", None, None), check_vma=False
    )
```

profile of v0, /device:TPU:6, one launch (start us, length us, event | category | flops | bytes accessed | tf_op | source)
XLA Modules:
  0.0 111.9 jit_solution(17206110789447896916)
XLA Ops:
  0.0 1.1 multiply_reduce_fusion
  1.1 1.2 %multiply_convert_fusion = bf16[1,2,160,384]{3,2,1,0:T(8,128)(2,1)S(1)} fusion(bf16[1,2,160,384]{3,2,1,0:T(8,128)(2,1)} %param.8, f32[384]{0:T(512)} %param.9, f32[2,160]{1,0:T(2,128)S(1)} %add_rsqrt_fusion), kind=kLoop, calls=%fused_computation.55 | loop fusion | flops 983040 | bytes 494336 | tf_op jit(solution)/shard_map/convert_element_type | solution.py:30
  2.3 3.8 %collective-permute-start = (bf16[1,2,160,384]{3,2,1,0:T(8,128)(2,1)S(1)}, bf16[1,2,160,384]{3,2,1,0:T(8,128)(2,1)S(1)}, u32[]{:S(2)}, u32[]{:S(2)}) collective-permute-start(bf16[1,2,160,384]{3,2,1,0:T(8,128)(2,1)S(1)} %multiply_convert_fusion), channel_id=1, source_target_pairs={{0,16},{8,24},{16,32},{24,40},{32,48},{40,56},{48,64},{56,72},{64,... | collective-permute-start | bytes 737288 | tf_op jit(solution)/shard_map/ppermute | solution.py:10
  6.1 1.9 %collective-permute-start.1 = (bf16[1,2,160,384]{3,2,1,0:T(8,128)(2,1)S(1)}, bf16[1,2,160,384]{3,2,1,0:T(8,128)(2,1)S(1)}, u32[]{:S(2)}, u32[]{:S(2)}) collective-permute-start(bf16[1,2,160,384]{3,2,1,0:T(8,128)(2,1)S(1)} %multiply_convert_fusion), channel_id=1, source_target_pairs={{0,8},{8,16},{16,24},{24,32},{32,40},{40,48},{48,56},{56,64},{64,7... | collective-permute-start | bytes 737288 | tf_op jit(solution)/shard_map/ppermute | solution.py:10
  8.1 0.8 fusion.45
  8.8 8.9 %collective-permute-done = bf16[1,2,160,384]{3,2,1,0:T(8,128)(2,1)S(1)} collective-permute-done((bf16[1,2,160,384]{3,2,1,0:T(8,128)(2,1)S(1)}, bf16[1,2,160,384]{3,2,1,0:T(8,128)(2,1)S(1)}, u32[]{:S(2)}, u32[]{:S(2)}) %collective-permute-start) | collective-permute-done | bytes 245792 | tf_op jit(solution)/shard_map/ppermute | solution.py:10
  17.7 1.9 %collective-permute-done.1 = bf16[1,2,160,384]{3,2,1,0:T(8,128)(2,1)S(1)} collective-permute-done((bf16[1,2,160,384]{3,2,1,0:T(8,128)(2,1)S(1)}, bf16[1,2,160,384]{3,2,1,0:T(8,128)(2,1)S(1)}, u32[]{:S(2)}, u32[]{:S(2)}) %collective-permute-start.1) | collective-permute-done | bytes 245792 | tf_op jit(solution)/shard_map/ppermute | solution.py:10
  19.7 2.9 %collective-permute-start.2 = (bf16[3,1,160,384]{3,2,1,0:T(8,128)(2,1)S(1)}, bf16[3,1,160,384]{3,2,1,0:T(8,128)(2,1)S(1)}, u32[]{:S(2)}, u32[]{:S(2)}) collective-permute-start(bf16[3,1,160,384]{3,2,1,0:T(8,128)(2,1)S(1)} %get-tuple-element.35), channel_id=1, source_target_pairs={{0,1},{1,2},{2,3},{3,4},{4,5},{5,6},{6,7},{8,9},{9,10},{10,11},{11... | collective-permute-start | bytes 1105928 | tf_op jit(solution)/shard_map/ppermute | solution.py:20
  22.6 3.0 %collective-permute-start.3 = (bf16[3,1,160,384]{3,2,1,0:T(8,128)(2,1)S(1)}, bf16[3,1,160,384]{3,2,1,0:T(8,128)(2,1)S(1)}, u32[]{:S(2)}, u32[]{:S(2)}) collective-permute-start(bf16[3,1,160,384]{3,2,1,0:T(8,128)(2,1)S(1)} %get-tuple-element.36), channel_id=1, source_target_pairs={{1,0},{2,1},{3,2},{4,3},{5,4},{6,5},{7,6},{9,8},{10,9},{11,10},{12... | collective-permute-start | bytes 1105928 | tf_op jit(solution)/shard_map/ppermute | solution.py:21
  25.6 3.9 %fusion.32 = (bf16[1,1,3,384,384]{4,3,2,1,0:T(8,128)(2,1)S(1)}, bf16[1,1,3,384,384]{4,3,2,1,0:T(8,128)(2,1)S(1)}, bf16[1,1,3,384,384]{4,3,2,1,0:T(8,128)(2,1)S(1...) fusion(bf16[3,3,3,384,384]{4,3,2,1,0:T(8,128)(2,1)} %param.10), kind=kLoop, calls=%fused_computation.85 | loop fusion | bytes 15925248 | tf_op jit(solution)/shard_map/slice | solution.py:54
  29.6 1.5 %collective-permute-done.2 = bf16[3,1,160,384]{3,2,1,0:T(8,128)(2,1)S(1)} collective-permute-done((bf16[3,1,160,384]{3,2,1,0:T(8,128)(2,1)S(1)}, bf16[3,1,160,384]{3,2,1,0:T(8,128)(2,1)S(1)}, u32[]{:S(2)}, u32[]{:S(2)}) %collective-permute-start.2) | collective-permute-done | bytes 368672 | tf_op jit(solution)/shard_map/ppermute | solution.py:20
  31.1 6.5 %collective-permute-done.3 = bf16[3,1,160,384]{3,2,1,0:T(8,128)(2,1)S(1)} collective-permute-done((bf16[3,1,160,384]{3,2,1,0:T(8,128)(2,1)S(1)}, bf16[3,1,160,384]{3,2,1,0:T(8,128)(2,1)S(1)}, u32[]{:S(2)}, u32[]{:S(2)}) %collective-permute-start.3) | collective-permute-done | bytes 368672 | tf_op jit(solution)/shard_map/ppermute | solution.py:21
  37.6 0.4 select_maximum_fusion
  39.6 0.6 fusion.46
  40.8 0.6 convolution_add_fusion.9
  41.4 0.6 convolution_add_fusion.8
  42.0 0.6 convolution_add_fusion.7
  42.6 0.6 convolution_add_fusion.6
  43.2 0.6 convolution_add_fusion.5
  43.8 0.6 convolution_add_fusion.4
  44.4 0.6 convolution_add_fusion.3
  45.0 0.6 fusion.14
  45.7 1.9 %collective-permute-start.5 = (bf16[1,2,160,384]{3,2,1,0:T(8,128)(2,1)S(1)}, bf16[1,2,160,384]{3,2,1,0:T(8,128)(2,1)S(1)}, u32[]{:S(2)}, u32[]{:S(2)}) collective-permute-start(bf16[1,2,160,384]{3,2,1,0:T(8,128)(2,1)S(1)} %add_convert_fusion), channel_id=1, source_target_pairs={{0,8},{8,16},{16,24},{24,32},{32,40},{40,48},{48,56},{56,64},{64,7... | collective-permute-start | bytes 737288 | tf_op jit(solution)/shard_map/ppermute | solution.py:10
  47.6 1.9 %collective-permute-start.4 = (bf16[1,2,160,384]{3,2,1,0:T(8,128)(2,1)S(1)}, bf16[1,2,160,384]{3,2,1,0:T(8,128)(2,1)S(1)}, u32[]{:S(2)}, u32[]{:S(2)}) collective-permute-start(bf16[1,2,160,384]{3,2,1,0:T(8,128)(2,1)S(1)} %add_convert_fusion), channel_id=1, source_target_pairs={{0,16},{8,24},{16,32},{24,40},{32,48},{40,56},{48,64},{56,72},{64,... | collective-permute-start | bytes 737288 | tf_op jit(solution)/shard_map/ppermute | solution.py:10
  50.2 6.7 %collective-permute-done.5 = bf16[1,2,160,384]{3,2,1,0:T(8,128)(2,1)S(1)} collective-permute-done((bf16[1,2,160,384]{3,2,1,0:T(8,128)(2,1)S(1)}, bf16[1,2,160,384]{3,2,1,0:T(8,128)(2,1)S(1)}, u32[]{:S(2)}, u32[]{:S(2)}) %collective-permute-start.5) | collective-permute-done | bytes 245792 | tf_op jit(solution)/shard_map/ppermute | solution.py:10
  57.5 4.5 %collective-permute-done.4 = bf16[1,2,160,384]{3,2,1,0:T(8,128)(2,1)S(1)} collective-permute-done((bf16[1,2,160,384]{3,2,1,0:T(8,128)(2,1)S(1)}, bf16[1,2,160,384]{3,2,1,0:T(8,128)(2,1)S(1)}, u32[]{:S(2)}, u32[]{:S(2)}) %collective-permute-start.4) | collective-permute-done | bytes 245792 | tf_op jit(solution)/shard_map/ppermute | solution.py:10
  62.4 0.3 fusion.12
  62.8 2.9 %collective-permute-start.6 = (bf16[2,1,160,384]{3,2,1,0:T(8,128)(2,1)S(1)}, bf16[2,1,160,384]{3,2,1,0:T(8,128)(2,1)S(1)}, u32[]{:S(2)}, u32[]{:S(2)}) collective-permute-start(bf16[2,1,160,384]{3,2,1,0:T(8,128)(2,1)S(1)} %get-tuple-element.37), channel_id=1, source_target_pairs={{0,1},{1,2},{2,3},{3,4},{4,5},{5,6},{6,7},{8,9},{9,10},{10,11},{11... | collective-permute-start | bytes 737288 | tf_op jit(solution)/shard_map/ppermute | solution.py:20
  65.7 3.2 %collective-permute-start.7 = (bf16[2,1,160,384]{3,2,1,0:T(8,128)(2,1)S(1)}, bf16[2,1,160,384]{3,2,1,0:T(8,128)(2,1)S(1)}, u32[]{:S(2)}, u32[]{:S(2)}) collective-permute-start(bf16[2,1,160,384]{3,2,1,0:T(8,128)(2,1)S(1)} %get-tuple-element.38), channel_id=1, source_target_pairs={{1,0},{2,1},{3,2},{4,3},{5,4},{6,5},{7,6},{9,8},{10,9},{11,10},{12... | collective-permute-start | bytes 737288 | tf_op jit(solution)/shard_map/ppermute | solution.py:21
  69.0 0.4 copy.10
  69.5 0.4 copy.11
  69.9 0.4 copy.12
  70.4 2.3 %collective-permute-done.6 = bf16[2,1,160,384]{3,2,1,0:T(8,128)(2,1)S(1)} collective-permute-done((bf16[2,1,160,384]{3,2,1,0:T(8,128)(2,1)S(1)}, bf16[2,1,160,384]{3,2,1,0:T(8,128)(2,1)S(1)}, u32[]{:S(2)}, u32[]{:S(2)}) %collective-permute-start.6) | collective-permute-done | bytes 245792 | tf_op jit(solution)/shard_map/ppermute | solution.py:20
  72.6 6.3 %collective-permute-done.7 = bf16[2,1,160,384]{3,2,1,0:T(8,128)(2,1)S(1)} collective-permute-done((bf16[2,1,160,384]{3,2,1,0:T(8,128)(2,1)S(1)}, bf16[2,1,160,384]{3,2,1,0:T(8,128)(2,1)S(1)}, u32[]{:S(2)}, u32[]{:S(2)}) %collective-permute-start.7) | collective-permute-done | bytes 245792 | tf_op jit(solution)/shard_map/ppermute | solution.py:21
  79.3 3.5 %broadcast_in_dim.5 = bf16[2,8,160,2,384]{4,3,2,1,0:T(2,128)(2,1)} broadcast(bf16[2,8,160,384]{3,2,1,0:T(8,128)(2,1)S(1)} %bitcast.116), dimensions={0,1,2,4} | broadcast | bytes 5898240 | tf_op jit(solution)/shard_map/broadcast_in_dim | solution.py:83
  82.8 9.1 %reshape.100 = bf16[2,8,320,384]{3,2,1,0:T(8,128)(2,1)} reshape(bf16[2,8,160,2,384]{4,3,2,1,0:T(2,128)(2,1)} %broadcast_in_dim.5) | data formatting | bytes 7864320 | tf_op jit(solution)/shard_map/reshape | solution.py:83
  91.8 2.1 %copy-done = bf16[2,8,320,384]{3,2,1,0:T(8,128)(2,1)S(1)} copy-done((bf16[2,8,320,384]{3,2,1,0:T(8,128)(2,1)S(1)}, bf16[2,8,320,384]{3,2,1,0:T(8,128)(2,1)}, u32[]{:S(2)}) %copy-start) | copy-done | bytes 3932184
  93.9 0.9 fusion.33
  94.8 0.9 slice-done
  95.8 4.3 %pad_slice_fusion.1 = (bf16[2,4,320,384]{3,2,1,0:T(8,128)(2,1)S(1)}, bf16[2,4,320,384]{3,2,1,0:T(8,128)(2,1)S(1)}, bf16[2,4,320,384]{3,2,1,0:T(8,128)(2,1)S(1)},...) fusion(bf16[2,6,320,384]{3,2,1,0:T(8,128)(2,1)S(1)} %slice-done), kind=kLoop, calls=%fused_computation.18 | loop fusion | bytes 14745600 | tf_op jit(solution)/shard_map/slice | solution.py:89
  100.0 1.0 pad_maximum_fusion
  101.1 2.1 %fusion.47 = f32[2560,192]{0,1:T(8,128)S(1)} fusion(bf16[2560,1152]{1,0:T(8,128)(2,1)S(1)} %bitcast.115, bf16[1152,192]{0,1:T(8,128)(2,1)S(1)} %bitcast.145), kind=kOutput, calls=%fused_computation.100 | convolution fusion | flops 1132462080 | bytes 8306688 | tf_op jit(solution)/shard_map/dot_general | solution.py:91
  103.2 1.0 pad_maximum_fusion.2
  104.2 1.0 pad_maximum_fusion.1
  105.3 2.1 %convolution_add_fusion.1 = f32[2560,192]{0,1:T(8,128)S(1)} fusion(f32[2560,192]{0,1:T(8,128)S(1)} %fusion.47, bf16[2560,1152]{1,0:T(8,128)(2,1)S(1)} %bitcast.114, bf16[1152,192]{0,1:T(8,128)(2,1)S(1)} %bitcast.144), kind=kOutput, calls=%fused_computation.7 | convolution fusion | flops 1132953600 | bytes 10272768 | tf_op jit(solution)/shard_map/dot_general | solution.py:91
  107.4 2.1 %fusion.1 = bf16[2560,192]{0,1:T(8,128)(2,1)S(1)} fusion(f32[2560,192]{0,1:T(8,128)S(1)} %convolution_add_fusion.1, bf16[2560,1152]{1,0:T(8,128)(2,1)S(1)} %bitcast.117, bf16[1152,192]{0,1:T(8,128)(2,1)S(1)} %bitcast.150, f32[192]{0:T(256)S(1)} %copy-done.5), kind=kOutput, calls=%fused_computation.8 | convolution fusion | flops 1133936640 | bytes 9290496 | tf_op jit(solution)/shard_map/dot_general | solution.py:91
  109.5 1.2 %reshape.104 = bf16[2,4,320,192]{2,1,0,3:T(4,128)(2,1)S(1)} reshape(bf16[2560,192]{0,1:T(8,128)(2,1)S(1)} %fusion.1) | data formatting | bytes 1966080 | tf_op jit(solution)/shard_map/reshape | solution.py:96
  110.8 1.2 %copy.13 = bf16[2,4,320,192]{2,3,1,0:T(8,128)(2,1)} copy(bf16[2,4,320,192]{2,1,0,3:T(4,128)(2,1)S(1)} %reshape.104) | data formatting | bytes 1966080 | tf_op jit(solution)/shard_map/reshape | solution.py:96
  (43 shorter events, 4.7 us)
Async XLA Ops:
  2.3 15.4 %collective-permute-start = (bf16[1,2,160,384]{3,2,1,0:T(8,128)(2,1)S(1)}, bf16[1,2,160,384]{3,2,1,0:T(8,128)(2,1)S(1)}, u32[]{:S(2)}, u32[]{:S(2)}) collective-permute-start(bf16[1,2,160,384]{3,2,1,0:T(8,128)(2,1)S(1)} %multiply_convert_fusion), channel_id=1, source_target_pairs={{0,16},{8,24},{16,32},{24,40},{32,48},{40,56},{48,64},{56,72},{64,... | collective-permute-start | bytes 737288 | tf_op jit(solution)/shard_map/ppermute | solution.py:10
  6.1 13.4 %collective-permute-start.1 = (bf16[1,2,160,384]{3,2,1,0:T(8,128)(2,1)S(1)}, bf16[1,2,160,384]{3,2,1,0:T(8,128)(2,1)S(1)}, u32[]{:S(2)}, u32[]{:S(2)}) collective-permute-start(bf16[1,2,160,384]{3,2,1,0:T(8,128)(2,1)S(1)} %multiply_convert_fusion), channel_id=1, source_target_pairs={{0,8},{8,16},{16,24},{24,32},{32,40},{40,48},{48,56},{56,64},{64,7... | collective-permute-start | bytes 737288 | tf_op jit(solution)/shard_map/ppermute | solution.py:10
  19.7 11.4 %collective-permute-start.2 = (bf16[3,1,160,384]{3,2,1,0:T(8,128)(2,1)S(1)}, bf16[3,1,160,384]{3,2,1,0:T(8,128)(2,1)S(1)}, u32[]{:S(2)}, u32[]{:S(2)}) collective-permute-start(bf16[3,1,160,384]{3,2,1,0:T(8,128)(2,1)S(1)} %get-tuple-element.35), channel_id=1, source_target_pairs={{0,1},{1,2},{2,3},{3,4},{4,5},{5,6},{6,7},{8,9},{9,10},{10,11},{11... | collective-permute-start | bytes 1105928 | tf_op jit(solution)/shard_map/ppermute | solution.py:20
  22.6 15.0 %collective-permute-start.3 = (bf16[3,1,160,384]{3,2,1,0:T(8,128)(2,1)S(1)}, bf16[3,1,160,384]{3,2,1,0:T(8,128)(2,1)S(1)}, u32[]{:S(2)}, u32[]{:S(2)}) collective-permute-start(bf16[3,1,160,384]{3,2,1,0:T(8,128)(2,1)S(1)} %get-tuple-element.36), channel_id=1, source_target_pairs={{1,0},{2,1},{3,2},{4,3},{5,4},{6,5},{7,6},{9,8},{10,9},{11,10},{12... | collective-permute-start | bytes 1105928 | tf_op jit(solution)/shard_map/ppermute | solution.py:21
  43.8 1.2 %copy-start.1 = (bf16[1,2,160,384]{3,2,1,0:T(8,128)(2,1)S(1)}, bf16[1,2,160,384]{3,2,1,0:T(8,128)(2,1)}, u32[]{:S(2)}) copy-start(bf16[1,2,160,384]{3,2,1,0:T(8,128)(2,1)} %param.8) | copy-start | bytes 737284
  43.8 1.2 %copy-start.4 = (f32[384]{0:T(512)S(1)}, f32[384]{0:T(512)}, u32[]{:S(2)}) copy-start(f32[384]{0:T(512)} %param.11) | copy-start | bytes 4612
  45.0 4.5 %copy-start.2 = (bf16[3,384,768]{2,1,0:T(8,128)(2,1)S(1)}, bf16[3,384,768]{2,1,0:T(8,128)(2,1)}, u32[]{:S(2)}) copy-start(bf16[3,384,768]{2,1,0:T(8,128)(2,1)} %param.12) | copy-start | bytes 5308420
  45.7 11.2 %collective-permute-start.5 = (bf16[1,2,160,384]{3,2,1,0:T(8,128)(2,1)S(1)}, bf16[1,2,160,384]{3,2,1,0:T(8,128)(2,1)S(1)}, u32[]{:S(2)}, u32[]{:S(2)}) collective-permute-start(bf16[1,2,160,384]{3,2,1,0:T(8,128)(2,1)S(1)} %add_convert_fusion), channel_id=1, source_target_pairs={{0,8},{8,16},{16,24},{24,32},{32,40},{40,48},{48,56},{56,64},{64,7... | collective-permute-start | bytes 737288 | tf_op jit(solution)/shard_map/ppermute | solution.py:10
  47.6 14.4 %collective-permute-start.4 = (bf16[1,2,160,384]{3,2,1,0:T(8,128)(2,1)S(1)}, bf16[1,2,160,384]{3,2,1,0:T(8,128)(2,1)S(1)}, u32[]{:S(2)}, u32[]{:S(2)}) collective-permute-start(bf16[1,2,160,384]{3,2,1,0:T(8,128)(2,1)S(1)} %add_convert_fusion), channel_id=1, source_target_pairs={{0,16},{8,24},{16,32},{24,40},{32,48},{40,56},{48,64},{56,72},{64,... | collective-permute-start | bytes 737288 | tf_op jit(solution)/shard_map/ppermute | solution.py:10
  62.0 6.8 %copy-start.3 = (bf16[3,3,384,192]{2,3,1,0:T(8,128)(2,1)S(1)}, bf16[3,3,384,192]{2,3,1,0:T(8,128)(2,1)}, u32[]{:S(2)}) copy-start(bf16[3,3,384,192]{2,3,1,0:T(8,128)(2,1)} %param.14) | copy-start | bytes 3981316
  62.8 9.8 %collective-permute-start.6 = (bf16[2,1,160,384]{3,2,1,0:T(8,128)(2,1)S(1)}, bf16[2,1,160,384]{3,2,1,0:T(8,128)(2,1)S(1)}, u32[]{:S(2)}, u32[]{:S(2)}) collective-permute-start(bf16[2,1,160,384]{3,2,1,0:T(8,128)(2,1)S(1)} %get-tuple-element.37), channel_id=1, source_target_pairs={{0,1},{1,2},{2,3},{3,4},{4,5},{5,6},{6,7},{8,9},{9,10},{10,11},{11... | collective-permute-start | bytes 737288 | tf_op jit(solution)/shard_map/ppermute | solution.py:20
  65.7 13.3 %collective-permute-start.7 = (bf16[2,1,160,384]{3,2,1,0:T(8,128)(2,1)S(1)}, bf16[2,1,160,384]{3,2,1,0:T(8,128)(2,1)S(1)}, u32[]{:S(2)}, u32[]{:S(2)}) collective-permute-start(bf16[2,1,160,384]{3,2,1,0:T(8,128)(2,1)S(1)} %get-tuple-element.38), channel_id=1, source_target_pairs={{1,0},{2,1},{3,2},{4,3},{5,4},{6,5},{7,6},{9,8},{10,9},{11,10},{12... | collective-permute-start | bytes 737288 | tf_op jit(solution)/shard_map/ppermute | solution.py:21
  91.8 2.1 %copy-start = (bf16[2,8,320,384]{3,2,1,0:T(8,128)(2,1)S(1)}, bf16[2,8,320,384]{3,2,1,0:T(8,128)(2,1)}, u32[]{:S(2)}) copy-start(bf16[2,8,320,384]{3,2,1,0:T(8,128)(2,1)} %reshape.100) | copy-start | bytes 11796484
  93.9 1.8 %slice-start = ((bf16[2,8,320,384]{3,2,1,0:T(8,128)(2,1)}), bf16[2,6,320,384]{3,2,1,0:T(8,128)(2,1)S(1)}, s32[]{:S(2)}) async-start(bf16[2,8,320,384]{3,2,1,0:T(8,128)(2,1)} %reshape.100), calls=%async_computation | async-start | bytes 5898240 | tf_op jit(solution)/shard_map/slice | solution.py:83
  105.3 2.1 %copy-start.5 = (f32[192]{0:T(256)S(1)}, f32[192]{0:T(256)}, u32[]{:S(2)}) copy-start(f32[192]{0:T(256)} %param.15) | copy-start | bytes 2308
where the time goes:
time: 113 us; the launch traced here: 112 us
  waiting for transfers between devices  38.5 us (34%)
  local copies, waits for them, and re-layouts  31.1 us (28%)
  starting transfers between devices  21.5 us (19%)
  matrix products  13.6 us (12%)
  other arithmetic  6.79 us (6%)
    ppermute x4, waiting for transfers between devices, shifted(): return lax.ppermute(block, axis, route)  21.9 us
    ppermute x2, waiting for transfers between devices, padded_2(): after = lax.ppermute(leading, axis, down)  12.8 us
    ppermute x4, starting transfers between devices, shifted(): return lax.ppermute(block, axis, route)  9.59 us
    reshape x1, local copies, waits for them, and re-layouts, upsample_conv(): jnp.repeat(jnp.repeat(edged, 2, axis=1), 2, axis=2)[:, 1:2 * rows_n + 3]  9.07 us
    dot_general x3, matrix products, upsample_conv(): jnp.dot(wide.reshape(-1, 3 * chans), up_weight[step_h].reshape(3 * chans,...  6.32 us
    ppermute x2, starting transfers between devices, padded_2(): after = lax.ppermute(leading, axis, down)  6.18 us
    ppermute x2, starting transfers between devices, padded_2(): before = lax.ppermute(last, axis, up)  5.71 us
    dot_general x9, matrix products, causal_conv(): jnp.dot(wide.reshape(-1, 3 * chans), conv_weight[step_t, step_h].reshape(...  5.3 us
  transfers between devices with their start and end apart: 8, of which 8 were waited for; matrix products, arithmetic and copies ran while one was open for 7% of the time, Pallas kernels for 0%

commit v1 on v0

v1 whole, which is shorter than its diff:
```python
import functools

import jax
import jax.numpy as jnp
from jax import lax
from jax.experimental import pallas as pl
from jax.experimental.pallas import tpu as pltpu
from jax.sharding import PartitionSpec as P

F32 = jnp.float32
BF16 = jnp.bfloat16
MESH = pl.DeviceIdType.MESH


def column_shift(flat, cols, step):
    total = flat.shape[0]
    rolled = pltpu.roll(flat, step % total, 0)
    place = lax.broadcasted_iota(jnp.int32, flat.shape, 0) % cols
    edge = 0 if step > 0 else cols - 1
    return jnp.where(place == edge, 0.0, rolled)


def kernel(
    frames, tiles,
    lat_hbm, gain_ref, cb_ref, tb_ref, ub_ref, cw_hbm, tw_hbm, uw_hbm,
    out_ref,
    lat, act, act_hist, parts, part_in, blk, blk_hist, dbl,
    cw, tw, uw, umat, acc, wide_lo, wide_hi,
    lat_sem, cw_sem, tw_sem, uw_sem,
    a_send, a_recv, a_fsend, b_send, b_recv, b_fsend,
    p_send, p_recv, d_send, d_recv,
):
    rows, cols, chans = lat.shape
    outs_n = uw.shape[2]
    low = 128
    high = outs_n - low
    cells = rows * cols
    t = lax.axis_index("tm")
    s = lax.axis_index("tile")
    odd = lax.rem(t, 2) == 1
    has_next = t + 2 < frames
    has_prev = t >= 2
    has_up = s > 0
    has_down = s < tiles - 1

    lat_copy = pltpu.make_async_copy(lat_hbm.at[0], lat, lat_sem)
    lat_copy.start()
    cw_copies = {}
    for dt in (2, 0, 1):
        for dh in range(3):
            copy = pltpu.make_async_copy(
                cw_hbm.at[dt, dh],
                cw.at[dt, :, :, pl.ds(dh * chans, chans)],
                cw_sem.at[dt, dh],
            )
            copy.start()
            cw_copies[dt, dh] = copy
    tw_copy = pltpu.make_async_copy(tw_hbm, tw, tw_sem)
    tw_copy.start()
    uw_copy = pltpu.make_async_copy(uw_hbm, uw, uw_sem)
    uw_copy.start()

    sibling = t + 1 - 2 * lax.rem(t, 2)
    barrier = pltpu.get_barrier_semaphore()

    def greet(condition, where):
        @pl.when(condition)
        def _():
            pl.semaphore_signal(barrier, inc=1, device_id=where, device_id_type=MESH)

    pl.semaphore_signal(barrier, inc=1, device_id={"tm": sibling}, device_id_type=MESH)
    greet(has_next, {"tm": t + 2})
    greet(has_prev, {"tm": t - 2})
    greet(has_up, {"tile": s - 1})
    greet(has_down, {"tile": s + 1})

    lat_copy.wait()
    for r in range(rows):
        values = lat[r].astype(F32)
        meansq = jnp.mean(values * values, axis=-1, keepdims=True)
        scaled = values * lax.rsqrt(meansq + 1e-06) * gain_ref[...]
        act[r] = (scaled * jax.nn.sigmoid(scaled)).astype(BF16)

    peers = 1
    for condition in (has_next, has_prev, has_up, has_down):
        peers = peers + condition.astype(jnp.int32)
    pl.semaphore_wait(barrier, peers)

    def history_copies(own, hist, send, recv, fsend):
        def nearer(r):
            return pltpu.make_async_remote_copy(
                own.at[r], hist.at[1, r], send.at[0, r], recv.at[1, r],
                device_id={"tm": sibling}, device_id_type=MESH,
            )

        def farther(r):
            return pltpu.make_async_remote_copy(
                own.at[r], hist.at[0, r], send.at[1, r], recv.at[0, r],
                device_id={"tm": t + 2}, device_id_type=MESH,
            )

        def forward(r):
            return pltpu.make_async_remote_copy(
                hist.at[0, r], hist.at[1, r], fsend.at[r], recv.at[1, r],
                device_id={"tm": sibling}, device_id_type=MESH,
            )

        return nearer, farther, forward

    def history_start(copies):
        nearer, farther, _ = copies
        for r in range(rows):
            @pl.when(has_next)
            def _():
                farther(r).start()

            @pl.when(jnp.logical_not(odd))
            def _():
                nearer(r).start()

    def history_far(copies, hist):
        _, farther, forward = copies

        @pl.when(has_prev)
        def _():
            for r in range(rows):
                farther(r).wait_recv()

                @pl.when(odd)
                def _():
                    forward(r).start()

        @pl.when(jnp.logical_not(has_prev))
        def _():
            hist[0] = jnp.zeros(hist.shape[1:], BF16)

    def history_near(copies, hist):
        nearer, _, _ = copies

        @pl.when(t >= 1)
        def _():
            for r in range(rows):
                nearer(r).wait_recv()

        @pl.when(t == 0)
        def _():
            hist[1] = jnp.zeros(hist.shape[1:], BF16)

    def history_end(copies):
        nearer, farther, forward = copies
        for r in range(rows):
            @pl.when(has_next)
            def _():
                farther(r).wait_send()

            @pl.when(jnp.logical_not(odd))
            def _():
                nearer(r).wait_send()

            @pl.when(jnp.logical_and(odd, has_prev))
            def _():
                forward(r).wait_send()

    def exchange(up_src, up_dst, down_src, down_dst, send, recv):
        up = pltpu.make_async_remote_copy(
            up_src, up_dst, send.at[0], recv.at[0], device_id={"tile": s - 1}, device_id_type=MESH
        )
        down = pltpu.make_async_remote_copy(
            down_src, down_dst, send.at[1], recv.at[1], device_id={"tile": s + 1}, device_id_type=MESH
        )

        @pl.when(has_up)
        def _():
            up.start()

        @pl.when(has_down)
        def _():
            down.start()

        return up, down

    act_copies = history_copies(act, act_hist, a_send, a_recv, a_fsend)
    history_start(act_copies)

    def conv_step(frame, dt):
        flat = frame.reshape(cells, chans)
        wide = flat.astype(F32)
        before = column_shift(wide, cols, 1).astype(BF16)
        after = column_shift(wide, cols, -1).astype(BF16)
        stacked = jnp.concatenate([before, flat, after], axis=1)
        for dh in range(3):
            cw_copies[dt, dh].wait()
        return jnp.dot(
            stacked, cw[dt].reshape(3 * chans, 3 * chans), preferred_element_type=F32
        )

    acc[...] = conv_step(act[...], 2)
    history_far(act_copies, act_hist)
    acc[...] += conv_step(act_hist[0], 0)
    history_near(act_copies, act_hist)
    acc[...] += conv_step(act_hist[1], 1)

    parts[0] = acc[pl.ds(0, cols), pl.ds(2 * chans, chans)].astype(BF16)
    parts[1] = acc[pl.ds(cells - cols, cols), pl.ds(0, chans)].astype(BF16)
    p_up, p_down = exchange(
        parts.at[0], part_in.at[1], parts.at[1], part_in.at[0], p_send, p_recv
    )

    def own_rows(r):
        total = acc[pl.ds(r * cols, cols), pl.ds(chans, chans)]
        if r > 0:
            total = total + acc[pl.ds((r - 1) * cols, cols), pl.ds(0, chans)]
        if r < rows - 1:
            total = total + acc[pl.ds((r + 1) * cols, cols), pl.ds(2 * chans, chans)]
        return total + cb_ref[...] + lat[r].astype(F32)

    @pl.when(has_up)
    def _():
        p_down.wait_recv()

    @pl.when(jnp.logical_not(has_up))
    def _():
        part_in[0] = jnp.zeros((cols, chans), BF16)

    @pl.when(has_down)
    def _():
        p_up.wait_recv()

    @pl.when(jnp.logical_not(has_down))
    def _():
        part_in[1] = jnp.zeros((cols, chans), BF16)

    for r in range(rows):
        total = own_rows(r)
        if r == 0:
            total = total + part_in[0].astype(F32)
        if r == rows - 1:
            total = total + part_in[1].astype(F32)
        blk[r] = total.astype(BF16)

    blk_copies = history_copies(blk, blk_hist, b_send, b_recv, b_fsend)
    history_start(blk_copies)

    uw_copy.wait()
    row_sets = {(0, 0): (0,), (0, 1): (1, 2), (1, 0): (0, 1), (1, 1): (2,)}
    for (a, i), picks in row_sets.items():
        taps = []
        for kw in range(3):
            tap = uw[picks[0], kw].astype(F32)
            for kh in picks[1:]:
                tap = tap + uw[kh, kw].astype(F32)
            taps.append(tap)
        center = (taps[1] + taps[2], taps[0] + taps[1])
        sides = (taps[0], taps[2])
        lanes = pl.ds(i * chans, chans)
        for base, pair in ((0, center), (2 * outs_n, sides)):
            for b in range(2):
                value = pair[b].astype(BF16)
                umat[a, pl.ds(base + b * low, low), lanes] = value[:low]
                umat[a, pl.ds(base + 2 * low + b * high, high), lanes] = value[low:]

    tw_copy.wait()

    def mix(frame, k):
        return jnp.dot(frame.reshape(cells, chans), tw[k], preferred_element_type=F32)

    mixed = mix(blk[...], 2) + tb_ref[...]
    history_far(blk_copies, blk_hist)
    mixed = mixed + mix(blk_hist[0], 0)
    history_near(blk_copies, blk_hist)
    mixed = (mixed + mix(blk_hist[1], 1)).astype(BF16)
    for r in range(rows):
        for f in range(2):
            dbl[1 + r, f] = mixed[r * cols : (r + 1) * cols, f * chans : (f + 1) * chans]

    d_up, d_down = exchange(
        dbl.at[1], dbl.at[rows + 1], dbl.at[rows], dbl.at[0], d_send, d_recv
    )

    def upsample_row(a, r):
        near = dbl[r + a].reshape(2 * cols, chans)
        far = dbl[r + a + 1].reshape(2 * cols, chans)
        both = jnp.concatenate([near, far], axis=1)
        result = lax.dot_general(
            both, umat[a], (((1,), (1,)), ((), ())), preferred_element_type=F32
        )
        center = result[:, : 2 * outs_n] + ub_ref[...]
        sides = result[:, 2 * outs_n :]
        even = center[:, :low] + column_shift(sides[:, :low], cols, 1)
        uneven = center[:, low : 2 * low] + column_shift(sides[:, low : 2 * low], cols, -1)
        tail = sides[:, 2 * low :]
        lane = lax.broadcasted_iota(jnp.int32, tail.shape, 1)
        tail = center[:, 2 * low :] + jnp.where(
            lane < high, column_shift(tail, cols, 1), column_shift(tail, cols, -1)
        )
        swapped = pltpu.roll(tail, high, 1)
        for f in range(2):
            span = slice(f * cols, (f + 1) * cols)
            wide_lo[pl.ds(0, cols, stride=2), :] = even[span]
            wide_lo[pl.ds(1, cols, stride=2), :] = uneven[span]
            wide_hi[pl.ds(0, cols, stride=2), :] = tail[span]
            wide_hi[pl.ds(1, cols, stride=2), :] = swapped[span]
            out_ref[f, 2 * r + a, :, pl.ds(0, low)] = wide_lo[...].astype(BF16)
            out_ref[f, 2 * r + a, :, pl.ds(low, high)] = wide_hi[:, :high].astype(BF16)

    for r in range(rows):
        for a in range(2):
            if 0 < r + a < rows:
                upsample_row(a, r)

    @pl.when(has_up)
    def _():
        d_down.wait_recv()

    @pl.when(jnp.logical_not(has_up))
    def _():
        dbl[0] = jnp.zeros(dbl.shape[1:], BF16)

    upsample_row(0, 0)

    @pl.when(has_down)
    def _():
        d_up.wait_recv()

    @pl.when(jnp.logical_not(has_down))
    def _():
        dbl[rows + 1] = jnp.zeros(dbl.shape[1:], BF16)

    upsample_row(1, rows - 1)

    history_end(act_copies)
    history_end(blk_copies)

    @pl.when(has_up)
    def _():
        p_up.wait_send()
        d_up.wait_send()

    @pl.when(has_down)
    def _():
        p_down.wait_send()
        d_down.wait_send()


def local(frames, tiles, latent, gain, conv_weight, conv_bias, time_weight, time_bias, up_weight, up_bias):
    _, rows, cols, chans = latent.shape
    outs_n = up_weight.shape[3]
    low, high = 128, outs_n - 128
    up_bias = jnp.concatenate([up_bias[:low], up_bias[:low], up_bias[low:], up_bias[low:]])
    vmem = pl.BlockSpec(memory_space=pltpu.VMEM)
    anywhere = pl.BlockSpec(memory_space=pl.ANY)
    dma = pltpu.SemaphoreType.DMA
    row = (cols, chans)
    return pl.pallas_call(
        functools.partial(kernel, frames, tiles),
        out_shape=jax.ShapeDtypeStruct((2, 2 * rows, 2 * cols, outs_n), BF16),
        in_specs=[anywhere, vmem, vmem, vmem, vmem, anywhere, anywhere, anywhere],
        out_specs=vmem,
        scratch_shapes=[
            pltpu.VMEM((rows,) + row, BF16),
            pltpu.VMEM((rows,) + row, BF16),
            pltpu.VMEM((2, rows) + row, BF16),
            pltpu.VMEM((2,) + row, BF16),
            pltpu.VMEM((2,) + row, BF16),
            pltpu.VMEM((rows,) + row, BF16),
            pltpu.VMEM((2, rows) + row, BF16),
            pltpu.VMEM((rows + 2, 2) + row, BF16),
            pltpu.VMEM((3, 3, chans, 3 * chans), BF16),
            pltpu.VMEM((3, chans, 2 * chans), BF16),
            pltpu.VMEM((3, 3, outs_n, chans), BF16),
            pltpu.VMEM((2, 4 * outs_n, 2 * chans), BF16),
            pltpu.VMEM((rows * cols, 3 * chans), F32),
            pltpu.VMEM((2 * cols, low), F32),
            pltpu.VMEM((2 * cols, low), F32),
            dma(()), dma((3, 3)), dma(()), dma(()),
            dma((2, rows)), dma((2, rows)), dma((rows,)),
            dma((2, rows)), dma((2, rows)), dma((rows,)),
            dma((2,)), dma((2,)), dma((2,)), dma((2,)),
        ],
        compiler_params=pltpu.CompilerParams(
            collective_id=0, has_side_effects=True, vmem_limit_bytes=60 * 1024 * 1024
        ),
    )(
        latent, gain[None], conv_bias[None], time_bias[None], up_bias[None],
        conv_weight, time_weight, jnp.swapaxes(up_weight, 2, 3),
    )


def solution(mesh):
    placed = (P("tm", "tile", None, None), P(), P(), P(), P(), P(), P(), P())
    return jax.shard_map(
        functools.partial(local, mesh.shape["tm"], mesh.shape["tile"]),
        mesh=mesh, in_specs=placed, out_specs=P("tm", "tile", None, None), check_vma=False,
    )
```

time: 113 us -> 55.5 us (0.49)
  the two profiles are of different devices: /device:TPU:6 before, /device:TPU:28 now
where the time goes in v1:
time: 55.5 us; the launch traced here: 55.2 us
  Pallas kernels  46.3 us (83%)
  local copies, waits for them, and re-layouts  8.15 us (15%)
  other arithmetic  0.75 us (1%)
    pallas_call x1, Pallas kernels, local(): pl.pallas_call(functools.partial(kernel, frames, tiles), out_shape=jax.Sh...  46.3 us
    pallas_call x1, local copies, waits for them, and re-layouts, local(): pl.pallas_call(functools.partial(kernel, frames, tiles), out_shape=jax.Sh...  2.47 us
    broadcast_in_dim x1, local copies, waits for them, and re-layouts, local(): time_bias[None]  1.27 us
    broadcast_in_dim x1, local copies, waits for them, and re-layouts, local(): conv_bias[None]  1.25 us
    broadcast_in_dim x1, local copies, waits for them, and re-layouts, local(): gain[None]  1.23 us

profile of v1, /device:TPU:28, one launch (start us, length us, event | category | flops | bytes accessed | tf_op | source)
XLA Modules:
  0.0 55.2 jit_solution(10694426188207411807)
XLA Ops:
  0.0 0.7 %slice.9 = f32[128]{0:T(128)S(1)} slice(f32[192]{0:T(256)} %param.15), slice={[0:128]} | slice | bytes 1024 | tf_op jit(solution)/shard_map/slice | solution.py:349
  0.7 0.7 %slice.10 = f32[64]{0:T(128)S(1)} slice(f32[192]{0:T(256)} %param.15), slice={[128:192]} | slice | bytes 512 | tf_op jit(solution)/shard_map/slice | solution.py:349
  1.4 0.8 %pad_maximum_fusion = f32[384]{0:T(512)S(1)} fusion(f32[64]{0:T(128)S(1)} %slice.10, f32[192]{0:T(256)} %param.15, f32[128]{0:T(128)S(1)} %slice.9), kind=kLoop, calls=%fused_computation | loop fusion | flops 768 | bytes 3072 | tf_op jit(solution)/shard_map/concatenate | solution.py:349
  2.1 0.6 %broadcast_in_dim.15.ub_ref = f32[1,384]{1,0:T(1,128)} reshape(f32[384]{0:T(512)S(1)} %pad_maximum_fusion) | data formatting | bytes 3072 | tf_op jit(solution)/shard_map/broadcast_in_dim | solution.py:384
  2.7 1.2 %broadcast_in_dim.12.gain_ref = f32[1,384]{1,0:T(1,128)} reshape(f32[384]{0:T(512)} %param.9) | data formatting | bytes 3072 | tf_op jit(solution)/shard_map/broadcast_in_dim | solution.py:384
  3.9 1.2 %broadcast_in_dim.13.cb_ref = f32[1,384]{1,0:T(1,128)} reshape(f32[384]{0:T(512)} %param.11) | data formatting | bytes 3072 | tf_op jit(solution)/shard_map/broadcast_in_dim | solution.py:384
  5.2 1.3 %broadcast_in_dim.14.tb_ref = f32[1,768]{1,0:T(1,128)} reshape(f32[768]{0:T(1024)} %param.13) | data formatting | bytes 6144 | tf_op jit(solution)/shard_map/broadcast_in_dim | solution.py:384
  6.4 46.3 %shard_map.82 = bf16[2,4,320,192]{3,2,1,0:T(8,128)(2,1)} custom-call(bf16[1,2,160,384]{3,2,1,0:T(8,128)(2,1)} %lat_hbm.1, f32[1,384]{1,0:T(1,128)} %broadcast_in_dim.12.gain_ref, f32[1,384]{1,0:T(1,128)} %broadcast_in_dim.13.cb_ref, f32[1,768]{1,0:T(1,128)} %broadcast_in_dim.14.tb_ref, f32[1,384]{1,0:T(1,128)} %broadcast_in_dim.15.ub_ref, ...), custom_call_target="tpu_custom_call" | custom-call | tf_op jit(solution)/shard_map/pallas_call | solution.py:354
  52.8 2.5 %copy.9 = bf16[2,4,320,192]{2,3,1,0:T(8,128)(2,1)} copy(bf16[2,4,320,192]{3,2,1,0:T(8,128)(2,1)} %shard_map.82) | data formatting | bytes 1966080 | tf_op jit(solution)/shard_map/pallas_call | solution.py:354

commit v2 on v1

--- a/solution.py
+++ b/solution.py
@@ -28,7 +28,7 @@
     cw, tw, uw, umat, acc, wide_lo, wide_hi,
     lat_sem, cw_sem, tw_sem, uw_sem,
     a_send, a_recv, a_fsend, b_send, b_recv, b_fsend,
-    p_send, p_recv, d_send, d_recv,
+    p_down_sem, p_up_sem, b_down_sem, d_up_sem,
 ):
     rows, cols, chans = lat.shape
     outs_n = uw.shape[2]
@@ -38,6 +38,7 @@
     t = lax.axis_index("tm")
     s = lax.axis_index("tile")
     odd = lax.rem(t, 2) == 1
+    even = jnp.logical_not(odd)
     has_next = t + 2 < frames
     has_prev = t >= 2
     has_up = s > 0
@@ -75,10 +76,10 @@
     greet(has_down, {"tile": s + 1})
 
     lat_copy.wait()
-    for r in range(rows):
+    for r in range(rows)[::-1]:
         values = lat[r].astype(F32)
         meansq = jnp.mean(values * values, axis=-1, keepdims=True)
-        scaled = values * lax.rsqrt(meansq + 1e-06) * gain_ref[...]
+        scaled = values * lax.rsqrt(meansq + 1e-06) * gain_ref[...].reshape(1, chans)
         act[r] = (scaled * jax.nn.sigmoid(scaled)).astype(BF16)
 
     peers = 1
@@ -107,139 +108,152 @@
 
         return nearer, farther, forward
 
-    def history_start(copies):
+    def history_start(copies, r):
         nearer, farther, _ = copies
-        for r in range(rows):
-            @pl.when(has_next)
+
+        @pl.when(has_next)
+        def _():
+            farther(r).start()
+
+        @pl.when(even)
+        def _():
+            nearer(r).start()
+
+    def history_far(copies, hist, r):
+        _, farther, forward = copies
+
+        @pl.when(has_prev)
+        def _():
+            farther(r).wait_recv()
+
+            @pl.when(odd)
             def _():
-                farther(r).start()
-
-            @pl.when(jnp.logical_not(odd))
-            def _():
-                nearer(r).start()
-
-    def history_far(copies, hist):
-        _, farther, forward = copies
-
-        @pl.when(has_prev)
-        def _():
-            for r in range(rows):
-                farther(r).wait_recv()
-
-                @pl.when(odd)
-                def _():
-                    forward(r).start()
+                forward(r).start()
 
         @pl.when(jnp.logical_not(has_prev))
         def _():
-            hist[0] = jnp.zeros(hist.shape[1:], BF16)
-
-    def history_near(copies, hist):
+            hist[0, r] = jnp.zeros(hist.shape[2:], BF16)
+
+    def history_near(copies, hist, r):
         nearer, _, _ = copies
 
         @pl.when(t >= 1)
         def _():
-            for r in range(rows):
-                nearer(r).wait_recv()
+            nearer(r).wait_recv()
 
         @pl.when(t == 0)
         def _():
-            hist[1] = jnp.zeros(hist.shape[1:], BF16)
-
-    def history_end(copies):
+            hist[1, r] = jnp.zeros(hist.shape[2:], BF16)
+
+    def history_end(copies, r):
         nearer, farther, forward = copies
-        for r in range(rows):
-            @pl.when(has_next)
-            def _():
-                farther(r).wait_send()
-
-            @pl.when(jnp.logical_not(odd))
-            def _():
-                nearer(r).wait_send()
-
-            @pl.when(jnp.logical_and(odd, has_prev))
-            def _():
-                forward(r).wait_send()
-
-    def exchange(up_src, up_dst, down_src, down_dst, send, recv):
-        up = pltpu.make_async_remote_copy(
-            up_src, up_dst, send.at[0], recv.at[0], device_id={"tile": s - 1}, device_id_type=MESH
+
+        @pl.when(has_next)
+        def _():
+            farther(r).wait_send()
+
+        @pl.when(even)
+        def _():
+            nearer(r).wait_send()
+
+        @pl.when(jnp.logical_and(odd, has_prev))
+        def _():
+            forward(r).wait_send()
+
+    def to_tile(src, dst, sems, where):
+        return pltpu.make_async_remote_copy(
+            src, dst, sems.at[0], sems.at[1], device_id={"tile": where}, device_id_type=MESH
         )
-        down = pltpu.make_async_remote_copy(
-            down_src, down_dst, send.at[1], recv.at[1], device_id={"tile": s + 1}, device_id_type=MESH
-        )
-
-        @pl.when(has_up)
-        def _():
-            up.start()
-
-        @pl.when(has_down)
-        def _():
-            down.start()
-
-        return up, down
-
+
+    first, last = 0, rows - 1
     act_copies = history_copies(act, act_hist, a_send, a_recv, a_fsend)
-    history_start(act_copies)
+    blk_copies = history_copies(blk, blk_hist, b_send, b_recv, b_fsend)
+    part_down = to_tile(parts.at[1], part_in.at[0], p_down_sem, s + 1)
+    part_up = to_tile(parts.at[0], part_in.at[1], p_up_sem, s - 1)
+    blk_down = to_tile(blk.at[rows], blk.at[0], b_down_sem, s + 1)
+    dbl_up = to_tile(dbl.at[1], dbl.at[rows + 1], d_up_sem, s - 1)
+
+    order = tuple(range(rows))[::-1]
+    for r in order:
+        history_start(act_copies, r)
 
     def conv_step(frame, dt):
-        flat = frame.reshape(cells, chans)
+        flat = frame.reshape(-1, chans)
         wide = flat.astype(F32)
         before = column_shift(wide, cols, 1).astype(BF16)
         after = column_shift(wide, cols, -1).astype(BF16)
         stacked = jnp.concatenate([before, flat, after], axis=1)
-        for dh in range(3):
-            cw_copies[dt, dh].wait()
         return jnp.dot(
             stacked, cw[dt].reshape(3 * chans, 3 * chans), preferred_element_type=F32
         )
 
+    def weights_ready(dt):
+        for dh in range(3):
+            cw_copies[dt, dh].wait()
+
+    weights_ready(2)
     acc[...] = conv_step(act[...], 2)
-    history_far(act_copies, act_hist)
-    acc[...] += conv_step(act_hist[0], 0)
-    history_near(act_copies, act_hist)
-    acc[...] += conv_step(act_hist[1], 1)
-
-    parts[0] = acc[pl.ds(0, cols), pl.ds(2 * chans, chans)].astype(BF16)
-    parts[1] = acc[pl.ds(cells - cols, cols), pl.ds(0, chans)].astype(BF16)
-    p_up, p_down = exchange(
-        parts.at[0], part_in.at[1], parts.at[1], part_in.at[0], p_send, p_recv
-    )
-
-    def own_rows(r):
+    weights_ready(0)
+    weights_ready(1)
+    for r in order:
+        span = pl.ds(r * cols, cols)
+        history_far(act_copies, act_hist, r)
+        acc[span, :] += conv_step(act_hist[0, r], 0)
+        history_near(act_copies, act_hist, r)
+        acc[span, :] += conv_step(act_hist[1, r], 1)
+        if r == last:
+            parts[1] = acc[span, pl.ds(0, chans)].astype(BF16)
+
+            @pl.when(has_down)
+            def _():
+                part_down.start()
+        if r == first:
+            parts[0] = acc[span, pl.ds(2 * chans, chans)].astype(BF16)
+
+            @pl.when(has_up)
+            def _():
+                part_up.start()
+
+    def finish_row(r):
         total = acc[pl.ds(r * cols, cols), pl.ds(chans, chans)]
         if r > 0:
             total = total + acc[pl.ds((r - 1) * cols, cols), pl.ds(0, chans)]
         if r < rows - 1:
             total = total + acc[pl.ds((r + 1) * cols, cols), pl.ds(2 * chans, chans)]
-        return total + cb_ref[...] + lat[r].astype(F32)
+        total = total + cb_ref[...].reshape(1, chans) + lat[r].astype(F32)
+        if r == first:
+            total = total + part_in[0].astype(F32)
+        if r == last:
+            total = total + part_in[1].astype(F32)
+        blk[1 + r] = total.astype(BF16)
 
     @pl.when(has_up)
     def _():
-        p_down.wait_recv()
+        part_down.wait_recv()
 
     @pl.when(jnp.logical_not(has_up))
     def _():
         part_in[0] = jnp.zeros((cols, chans), BF16)
 
+    for r in range(rows - 1):
+        finish_row(r)
+        history_start(blk_copies, 1 + r)
+
     @pl.when(has_down)
     def _():
-        p_up.wait_recv()
+        part_up.wait_recv()
 
     @pl.when(jnp.logical_not(has_down))
     def _():
         part_in[1] = jnp.zeros((cols, chans), BF16)
 
-    for r in range(rows):
-        total = own_rows(r)
-        if r == 0:
-            total = total + part_in[0].astype(F32)
-        if r == rows - 1:
-            total = total + part_in[1].astype(F32)
-        blk[r] = total.astype(BF16)
-
-    blk_copies = history_copies(blk, blk_hist, b_send, b_recv, b_fsend)
-    history_start(blk_copies)
+    finish_row(last)
+
+    @pl.when(has_down)
+    def _():
+        blk_down.start()
+
+    history_start(blk_copies, rows)
 
     uw_copy.wait()
     row_sets = {(0, 0): (0,), (0, 1): (1, 2), (1, 0): (0, 1), (1, 1): (2,)}
@@ -261,20 +275,37 @@
 
     tw_copy.wait()
 
-    def mix(frame, k):
-        return jnp.dot(frame.reshape(cells, chans), tw[k], preferred_element_type=F32)
-
-    mixed = mix(blk[...], 2) + tb_ref[...]
-    history_far(blk_copies, blk_hist)
-    mixed = mixed + mix(blk_hist[0], 0)
-    history_near(blk_copies, blk_hist)
-    mixed = (mixed + mix(blk_hist[1], 1)).astype(BF16)
+    def mix(row, k):
+        return jnp.dot(row.reshape(-1, chans), tw[k], preferred_element_type=F32)
+
+    def mix_row(j, mixed):
+        mixed = mixed + mix(blk_hist[0, j], 0)
+        history_near(blk_copies, blk_hist, j)
+        mixed = (mixed + mix(blk_hist[1, j], 1)).astype(BF16)
+        for f in range(2):
+            dbl[j, f] = mixed[:, f * chans : (f + 1) * chans]
+
+    def newest(j):
+        return mix(blk[j], 2) + tb_ref[...].reshape(1, 2 * chans)
+
     for r in range(rows):
-        for f in range(2):
-            dbl[1 + r, f] = mixed[r * cols : (r + 1) * cols, f * chans : (f + 1) * chans]
-
-    d_up, d_down = exchange(
-        dbl.at[1], dbl.at[rows + 1], dbl.at[rows], dbl.at[0], d_send, d_recv
+        start = newest(1 + r)
+        if r == last:
+            @pl.when(has_up)
+            def _():
+                blk_down.wait_recv()
+                history_start(blk_copies, 0)
+
+        history_far(blk_copies, blk_hist, 1 + r)
+        mix_row(1 + r, start)
+        if r == first:
+            @pl.when(has_up)
+            def _():
+                dbl_up.start()
+
+    bias_row = ub_ref[...].reshape(1, outs_n)
+    up_bias = jnp.concatenate(
+        [bias_row[:, :low], bias_row[:, :low], bias_row[:, low:], bias_row[:, low:]], axis=1
     )
 
     def upsample_row(a, r):
@@ -284,7 +315,7 @@
         result = lax.dot_general(
             both, umat[a], (((1,), (1,)), ((), ())), preferred_element_type=F32
         )
-        center = result[:, : 2 * outs_n] + ub_ref[...]
+        center = result[:, : 2 * outs_n] + up_bias
         sides = result[:, 2 * outs_n :]
         even = center[:, :low] + column_shift(sides[:, :low], cols, 1)
         uneven = center[:, low : 2 * low] + column_shift(sides[:, low : 2 * low], cols, -1)
@@ -310,7 +341,8 @@
 
     @pl.when(has_up)
     def _():
-        d_down.wait_recv()
+        history_far(blk_copies, blk_hist, 0)
+        mix_row(0, newest(0))
 
     @pl.when(jnp.logical_not(has_up))
     def _():
@@ -320,35 +352,36 @@
 
     @pl.when(has_down)
     def _():
-        d_up.wait_recv()
+        dbl_up.wait_recv()
 
     @pl.when(jnp.logical_not(has_down))
     def _():
         dbl[rows + 1] = jnp.zeros(dbl.shape[1:], BF16)
 
-    upsample_row(1, rows - 1)
-
-    history_end(act_copies)
-    history_end(blk_copies)
+    upsample_row(1, last)
+
+    for r in range(rows):
+        history_end(act_copies, r)
+        history_end(blk_copies, 1 + r)
 
     @pl.when(has_up)
     def _():
-        p_up.wait_send()
-        d_up.wait_send()
+        history_end(blk_copies, 0)
+        part_up.wait_send()
+        dbl_up.wait_send()
 
     @pl.when(has_down)
     def _():
-        p_down.wait_send()
-        d_down.wait_send()
+        part_down.wait_send()
+        blk_down.wait_send()
 
 
 def local(frames, tiles, latent, gain, conv_weight, conv_bias, time_weight, time_bias, up_weight, up_bias):
     _, rows, cols, chans = latent.shape
     outs_n = up_weight.shape[3]
-    low, high = 128, outs_n - 128
-    up_bias = jnp.concatenate([up_bias[:low], up_bias[:low], up_bias[low:], up_bias[low:]])
+    low = 128
     vmem = pl.BlockSpec(memory_space=pltpu.VMEM)
-    anywhere = pl.BlockSpec(memory_space=pl.ANY)
+    anywhere = pl.BlockSpec(memory_space=pltpu.HBM)
     dma = pltpu.SemaphoreType.DMA
     row = (cols, chans)
     return pl.pallas_call(
@@ -362,8 +395,8 @@
             pltpu.VMEM((2, rows) + row, BF16),
             pltpu.VMEM((2,) + row, BF16),
             pltpu.VMEM((2,) + row, BF16),
-            pltpu.VMEM((rows,) + row, BF16),
-            pltpu.VMEM((2, rows) + row, BF16),
+            pltpu.VMEM((rows + 1,) + row, BF16),
+            pltpu.VMEM((2, rows + 1) + row, BF16),
             pltpu.VMEM((rows + 2, 2) + row, BF16),
             pltpu.VMEM((3, 3, chans, 3 * chans), BF16),
             pltpu.VMEM((3, chans, 2 * chans), BF16),
@@ -374,14 +407,14 @@
             pltpu.VMEM((2 * cols, low), F32),
             dma(()), dma((3, 3)), dma(()), dma(()),
             dma((2, rows)), dma((2, rows)), dma((rows,)),
-            dma((2, rows)), dma((2, rows)), dma((rows,)),
+            dma((2, rows + 1)), dma((2, rows + 1)), dma((rows + 1,)),
             dma((2,)), dma((2,)), dma((2,)), dma((2,)),
         ],
         compiler_params=pltpu.CompilerParams(
             collective_id=0, has_side_effects=True, vmem_limit_bytes=60 * 1024 * 1024
         ),
     )(
-        latent, gain[None], conv_bias[None], time_bias[None], up_bias[None],
+        latent, gain, conv_bias, time_bias, up_bias,
         conv_weight, time_weight, jnp.swapaxes(up_weight, 2, 3),
     )
 

time: 55.5 us -> 41.7 us (0.75)
  the two profiles are of different devices: /device:TPU:28 before, /device:TPU:50 now
where the time goes in v2:
time: 41.7 us; the launch traced here: 41.6 us
  Pallas kernels  39.1 us (94%)
  local copies, waits for them, and re-layouts  2.47 us (6%)
    pallas_call x1, Pallas kernels, local(): pl.pallas_call(functools.partial(kernel, frames, tiles), out_shape=jax.Sh...  39.1 us
    pallas_call x1, local copies, waits for them, and re-layouts, local(): pl.pallas_call(functools.partial(kernel, frames, tiles), out_shape=jax.Sh...  2.47 us

profile of v2, /device:TPU:50, one launch (start us, length us, event | category | flops | bytes accessed | tf_op | source)
XLA Modules:
  0.0 41.6 jit_solution(363533328542752588)
XLA Ops:
  0.0 39.1 %shard_map.82 = bf16[2,4,320,192]{3,2,1,0:T(8,128)(2,1)} custom-call(bf16[1,2,160,384]{3,2,1,0:T(8,128)(2,1)} %lat_hbm.1, f32[384]{0:T(512)} %gain_ref.1, f32[384]{0:T(512)} %cb_ref.1, f32[768]{0:T(1024)} %tb_ref.1, f32[192]{0:T(256)} %ub_ref.1, bf16[3,3,3,384,384]{4,3,2,1,0:T(8,128)(2,1)} %cw_hbm.1, bf16[3,384,768]{2,1,0:T(8,128)(2,1)} %tw_hbm.1, ...), custom_call_target="tpu_custom_call" | custom-call | tf_op jit(solution)/shard_map/pallas_call | solution.py:387
  39.1 2.5 %copy.9 = bf16[2,4,320,192]{2,3,1,0:T(8,128)(2,1)} copy(bf16[2,4,320,192]{3,2,1,0:T(8,128)(2,1)} %shard_map.82) | data formatting | bytes 1966080 | tf_op jit(solution)/shard_map/pallas_call | solution.py:387

commit v3 on v2

--- a/solution.py
+++ b/solution.py
@@ -25,7 +25,7 @@
     lat_hbm, gain_ref, cb_ref, tb_ref, ub_ref, cw_hbm, tw_hbm, uw_hbm,
     out_ref,
     lat, act, act_hist, parts, part_in, blk, blk_hist, dbl,
-    cw, tw, uw, umat, acc, wide_lo, wide_hi,
+    cw, tw, uw, umat, acc, mixed, edge, wide_lo, wide_hi,
     lat_sem, cw_sem, tw_sem, uw_sem,
     a_send, a_recv, a_fsend, b_send, b_recv, b_fsend,
     p_down_sem, p_up_sem, b_down_sem, d_up_sem,
@@ -41,6 +41,7 @@
     even = jnp.logical_not(odd)
     has_next = t + 2 < frames
     has_prev = t >= 2
+    has_near = t >= 1
     has_up = s > 0
     has_down = s < tiles - 1
 
@@ -75,18 +76,6 @@
     greet(has_up, {"tile": s - 1})
     greet(has_down, {"tile": s + 1})
 
-    lat_copy.wait()
-    for r in range(rows)[::-1]:
-        values = lat[r].astype(F32)
-        meansq = jnp.mean(values * values, axis=-1, keepdims=True)
-        scaled = values * lax.rsqrt(meansq + 1e-06) * gain_ref[...].reshape(1, chans)
-        act[r] = (scaled * jax.nn.sigmoid(scaled)).astype(BF16)
-
-    peers = 1
-    for condition in (has_next, has_prev, has_up, has_down):
-        peers = peers + condition.astype(jnp.int32)
-    pl.semaphore_wait(barrier, peers)
-
     def history_copies(own, hist, send, recv, fsend):
         def nearer(r):
             return pltpu.make_async_remote_copy(
@@ -119,31 +108,16 @@
         def _():
             nearer(r).start()
 
-    def history_far(copies, hist, r):
+    def history_far(copies, r):
         _, farther, forward = copies
-
-        @pl.when(has_prev)
-        def _():
-            farther(r).wait_recv()
-
-            @pl.when(odd)
-            def _():
-                forward(r).start()
-
-        @pl.when(jnp.logical_not(has_prev))
-        def _():
-            hist[0, r] = jnp.zeros(hist.shape[2:], BF16)
-
-    def history_near(copies, hist, r):
-        nearer, _, _ = copies
-
-        @pl.when(t >= 1)
-        def _():
-            nearer(r).wait_recv()
-
-        @pl.when(t == 0)
-        def _():
-            hist[1, r] = jnp.zeros(hist.shape[2:], BF16)
+        farther(r).wait_recv()
+
+        @pl.when(odd)
+        def _():
+            forward(r).start()
+
+    def history_near(copies, r):
+        copies[0](r).wait_recv()
 
     def history_end(copies, r):
         nearer, farther, forward = copies
@@ -173,46 +147,71 @@
     blk_down = to_tile(blk.at[rows], blk.at[0], b_down_sem, s + 1)
     dbl_up = to_tile(dbl.at[1], dbl.at[rows + 1], d_up_sem, s - 1)
 
+    def activate(r):
+        values = lat[r].astype(F32)
+        meansq = jnp.mean(values * values, axis=-1, keepdims=True)
+        scaled = values * lax.rsqrt(meansq + 1e-06) * gain_ref[...].reshape(1, chans)
+        act[r] = (scaled * jax.nn.sigmoid(scaled)).astype(BF16)
+
+    peers = 1
+    for condition in (has_next, has_prev, has_up, has_down):
+        peers = peers + condition.astype(jnp.int32)
+
     order = tuple(range(rows))[::-1]
+    lat_copy.wait()
     for r in order:
+        activate(r)
+        if r == order[0]:
+            pl.semaphore_wait(barrier, peers)
         history_start(act_copies, r)
 
-    def conv_step(frame, dt):
+    def widen(frame):
         flat = frame.reshape(-1, chans)
         wide = flat.astype(F32)
         before = column_shift(wide, cols, 1).astype(BF16)
         after = column_shift(wide, cols, -1).astype(BF16)
-        stacked = jnp.concatenate([before, flat, after], axis=1)
-        return jnp.dot(
-            stacked, cw[dt].reshape(3 * chans, 3 * chans), preferred_element_type=F32
-        )
+        return jnp.concatenate([before, flat, after], axis=1)
+
+    def conv(stacked, dt, start, size):
+        taps = cw.at[dt, :, :, pl.ds(start, size)][...].reshape(3 * chans, size)
+        return jnp.dot(stacked, taps, preferred_element_type=F32)
 
     def weights_ready(dt):
         for dh in range(3):
             cw_copies[dt, dh].wait()
 
     weights_ready(2)
-    acc[...] = conv_step(act[...], 2)
+    acc[...] = conv(widen(act[...]), 2, 0, 3 * chans)
     weights_ready(0)
     weights_ready(1)
     for r in order:
         span = pl.ds(r * cols, cols)
-        history_far(act_copies, act_hist, r)
-        acc[span, :] += conv_step(act_hist[0, r], 0)
-        history_near(act_copies, act_hist, r)
-        acc[span, :] += conv_step(act_hist[1, r], 1)
+        goes, stays = (0, chans) if r == last else (2 * chans, 0)
+        out_part = 1 if r == last else 0
+
+        @pl.when(has_prev)
+        def _():
+            history_far(act_copies, r)
+            acc[span, :] += conv(widen(act_hist[0, r]), 0, 0, 3 * chans)
+
+        @pl.when(has_near)
+        def _():
+            history_near(act_copies, r)
+            acc[span, pl.ds(goes, chans)] += conv(widen(act_hist[1, r]), 1, goes, chans)
+
+        parts[out_part] = acc[span, pl.ds(goes, chans)].astype(BF16)
         if r == last:
-            parts[1] = acc[span, pl.ds(0, chans)].astype(BF16)
-
             @pl.when(has_down)
             def _():
                 part_down.start()
-        if r == first:
-            parts[0] = acc[span, pl.ds(2 * chans, chans)].astype(BF16)
-
+        else:
             @pl.when(has_up)
             def _():
                 part_up.start()
+
+        @pl.when(has_near)
+        def _():
+            acc[span, pl.ds(stays, 2 * chans)] += conv(widen(act_hist[1, r]), 1, stays, 2 * chans)
 
     def finish_row(r):
         total = acc[pl.ds(r * cols, cols), pl.ds(chans, chans)]
@@ -276,28 +275,35 @@
     tw_copy.wait()
 
     def mix(row, k):
-        return jnp.dot(row.reshape(-1, chans), tw[k], preferred_element_type=F32)
-
-    def mix_row(j, mixed):
-        mixed = mixed + mix(blk_hist[0, j], 0)
-        history_near(blk_copies, blk_hist, j)
-        mixed = (mixed + mix(blk_hist[1, j], 1)).astype(BF16)
+        return jnp.dot(row, tw[k], preferred_element_type=F32)
+
+    def newest(j):
+        mixed[j] = mix(blk[j], 2) + tb_ref[...].reshape(1, 2 * chans)
+
+    def mix_row(j):
+        @pl.when(has_prev)
+        def _():
+            history_far(blk_copies, j)
+            mixed[j] += mix(blk_hist[0, j], 0)
+
+        @pl.when(has_near)
+        def _():
+            history_near(blk_copies, j)
+            mixed[j] += mix(blk_hist[1, j], 1)
+
         for f in range(2):
-            dbl[j, f] = mixed[:, f * chans : (f + 1) * chans]
-
-    def newest(j):
-        return mix(blk[j], 2) + tb_ref[...].reshape(1, 2 * chans)
+            dbl[j, f] = mixed[j, :, pl.ds(f * chans, chans)].astype(BF16)
 
     for r in range(rows):
-        start = newest(1 + r)
+        newest(1 + r)
+    for r in range(rows):
         if r == last:
             @pl.when(has_up)
             def _():
                 blk_down.wait_recv()
                 history_start(blk_copies, 0)
 
-        history_far(blk_copies, blk_hist, 1 + r)
-        mix_row(1 + r, start)
+        mix_row(1 + r)
         if r == first:
             @pl.when(has_up)
             def _():
@@ -308,13 +314,15 @@
         [bias_row[:, :low], bias_row[:, :low], bias_row[:, low:], bias_row[:, low:]], axis=1
     )
 
-    def upsample_row(a, r):
-        near = dbl[r + a].reshape(2 * cols, chans)
-        far = dbl[r + a + 1].reshape(2 * cols, chans)
-        both = jnp.concatenate([near, far], axis=1)
-        result = lax.dot_general(
-            both, umat[a], (((1,), (1,)), ((), ())), preferred_element_type=F32
+    def taps_dot(row, a, start, size):
+        return lax.dot_general(
+            row, umat[a, :, pl.ds(start, size)], (((1,), (1,)), ((), ())), preferred_element_type=F32
         )
+
+    def stored_row(j):
+        return dbl[j].reshape(2 * cols, chans)
+
+    def upsample_row(a, r, result):
         center = result[:, : 2 * outs_n] + up_bias
         sides = result[:, 2 * outs_n :]
         even = center[:, :low] + column_shift(sides[:, :low], cols, 1)
@@ -337,28 +345,26 @@
     for r in range(rows):
         for a in range(2):
             if 0 < r + a < rows:
-                upsample_row(a, r)
+                both = jnp.concatenate([stored_row(r + a), stored_row(r + a + 1)], axis=1)
+                upsample_row(a, r, taps_dot(both, a, 0, 2 * chans))
+
+    edge[0] = taps_dot(stored_row(1), 0, chans, chans)
+    edge[1] = taps_dot(stored_row(rows), 1, 0, chans)
 
     @pl.when(has_up)
     def _():
-        history_far(blk_copies, blk_hist, 0)
-        mix_row(0, newest(0))
-
-    @pl.when(jnp.logical_not(has_up))
-    def _():
-        dbl[0] = jnp.zeros(dbl.shape[1:], BF16)
-
-    upsample_row(0, 0)
+        newest(0)
+        mix_row(0)
+        edge[0] += taps_dot(stored_row(0), 0, 0, chans)
+
+    upsample_row(0, 0, edge[0])
 
     @pl.when(has_down)
     def _():
         dbl_up.wait_recv()
-
-    @pl.when(jnp.logical_not(has_down))
-    def _():
-        dbl[rows + 1] = jnp.zeros(dbl.shape[1:], BF16)
-
-    upsample_row(1, last)
+        edge[1] += taps_dot(stored_row(rows + 1), 1, chans, chans)
+
+    upsample_row(1, last, edge[1])
 
     for r in range(rows):
         history_end(act_copies, r)
@@ -403,6 +409,8 @@
             pltpu.VMEM((3, 3, outs_n, chans), BF16),
             pltpu.VMEM((2, 4 * outs_n, 2 * chans), BF16),
             pltpu.VMEM((rows * cols, 3 * chans), F32),
+            pltpu.VMEM((rows + 1, cols, 2 * chans), F32),
+            pltpu.VMEM((2, 2 * cols, 4 * outs_n), F32),
             pltpu.VMEM((2 * cols, low), F32),
             pltpu.VMEM((2 * cols, low), F32),
             dma(()), dma((3, 3)), dma(()), dma(()),

time: 41.7 us -> 40.3 us (0.966)
  the two profiles are of different devices: /device:TPU:50 before, /device:TPU:10 now
where the time goes in v3:
time: 40.3 us; the launch traced here: 40.1 us
  Pallas kernels  37.7 us (94%)
  local copies, waits for them, and re-layouts  2.47 us (6%)
    pallas_call x1, Pallas kernels, local(): pl.pallas_call(functools.partial(kernel, frames, tiles), out_shape=jax.Sh...  37.7 us
    pallas_call x1, local copies, waits for them, and re-layouts, local(): pl.pallas_call(functools.partial(kernel, frames, tiles), out_shape=jax.Sh...  2.47 us

profile of v3, /device:TPU:10, one launch (start us, length us, event | category | flops | bytes accessed | tf_op | source)
XLA Modules:
  0.0 40.1 jit_solution(10283134489578695454)
XLA Ops:
  0.0 37.7 %shard_map.82 = bf16[2,4,320,192]{3,2,1,0:T(8,128)(2,1)} custom-call(bf16[1,2,160,384]{3,2,1,0:T(8,128)(2,1)} %lat_hbm.1, f32[384]{0:T(512)} %gain_ref.1, f32[384]{0:T(512)} %cb_ref.1, f32[768]{0:T(1024)} %tb_ref.1, f32[192]{0:T(256)} %ub_ref.1, bf16[3,3,3,384,384]{4,3,2,1,0:T(8,128)(2,1)} %cw_hbm.1, bf16[3,384,768]{2,1,0:T(8,128)(2,1)} %tw_hbm.1, ...), custom_call_target="tpu_custom_call" | custom-call | tf_op jit(solution)/shard_map/pallas_call | solution.py:393
  37.7 2.5 %copy.9 = bf16[2,4,320,192]{2,3,1,0:T(8,128)(2,1)} copy(bf16[2,4,320,192]{3,2,1,0:T(8,128)(2,1)} %shard_map.82) | data formatting | bytes 1966080 | tf_op jit(solution)/shard_map/pallas_call | solution.py:393

commit v4 on v3

--- a/solution.py
+++ b/solution.py
@@ -22,11 +22,11 @@
 
 def kernel(
     frames, tiles,
-    lat_hbm, gain_ref, cb_ref, tb_ref, ub_ref, cw_hbm, tw_hbm, uw_hbm,
+    lat_hbm, gain_hbm, cb_hbm, tb_hbm, ub_hbm, cw_hbm, tw_hbm, uw_hbm,
     out_ref,
     lat, act, act_hist, parts, part_in, blk, blk_hist, dbl,
-    cw, tw, uw, umat, acc, mixed, edge, wide_lo, wide_hi,
-    lat_sem, cw_sem, tw_sem, uw_sem,
+    gain_ref, cb_ref, tb_ref, ub_ref, cw, tw, uw, umat, acc, mixed, edge, wide_lo, wide_hi,
+    lat_sem, bias_sem, cw_sem, tw_sem, uw_sem,
     a_send, a_recv, a_fsend, b_send, b_recv, b_fsend,
     p_down_sem, p_up_sem, b_down_sem, d_up_sem,
 ):
@@ -47,6 +47,13 @@
 
     lat_copy = pltpu.make_async_copy(lat_hbm.at[0], lat, lat_sem)
     lat_copy.start()
+    bias_copies = []
+    for k, (src, dst) in enumerate(
+        ((gain_hbm, gain_ref), (cb_hbm, cb_ref), (tb_hbm, tb_ref), (ub_hbm, ub_ref))
+    ):
+        copy = pltpu.make_async_copy(src, dst, bias_sem.at[k])
+        copy.start()
+        bias_copies.append(copy)
     cw_copies = {}
     for dt in (2, 0, 1):
         for dh in range(3):
@@ -159,6 +166,8 @@
 
     order = tuple(range(rows))[::-1]
     lat_copy.wait()
+    for copy in bias_copies:
+        copy.wait()
     for r in order:
         activate(r)
         if r == order[0]:
@@ -386,15 +395,13 @@
     _, rows, cols, chans = latent.shape
     outs_n = up_weight.shape[3]
     low = 128
-    vmem = pl.BlockSpec(memory_space=pltpu.VMEM)
-    anywhere = pl.BlockSpec(memory_space=pltpu.HBM)
     dma = pltpu.SemaphoreType.DMA
     row = (cols, chans)
     return pl.pallas_call(
         functools.partial(kernel, frames, tiles),
         out_shape=jax.ShapeDtypeStruct((2, 2 * rows, 2 * cols, outs_n), BF16),
-        in_specs=[anywhere, vmem, vmem, vmem, vmem, anywhere, anywhere, anywhere],
-        out_specs=vmem,
+        in_specs=[pl.BlockSpec(memory_space=pltpu.HBM)] * 8,
+        out_specs=pl.BlockSpec(memory_space=pltpu.VMEM),
         scratch_shapes=[
             pltpu.VMEM((rows,) + row, BF16),
             pltpu.VMEM((rows,) + row, BF16),
@@ -404,6 +411,10 @@
             pltpu.VMEM((rows + 1,) + row, BF16),
             pltpu.VMEM((2, rows + 1) + row, BF16),
             pltpu.VMEM((rows + 2, 2) + row, BF16),
+            pltpu.VMEM((chans,), F32),
+            pltpu.VMEM((chans,), F32),
+            pltpu.VMEM((2 * chans,), F32),
+            pltpu.VMEM((outs_n,), F32),
             pltpu.VMEM((3, 3, chans, 3 * chans), BF16),
             pltpu.VMEM((3, chans, 2 * chans), BF16),
             pltpu.VMEM((3, 3, outs_n, chans), BF16),
@@ -413,18 +424,21 @@
             pltpu.VMEM((2, 2 * cols, 4 * outs_n), F32),
             pltpu.VMEM((2 * cols, low), F32),
             pltpu.VMEM((2 * cols, low), F32),
-            dma(()), dma((3, 3)), dma(()), dma(()),
+            dma(()), dma((4,)), dma((3, 3)), dma(()), dma(()),
             dma((2, rows)), dma((2, rows)), dma((rows,)),
             dma((2, rows + 1)), dma((2, rows + 1)), dma((rows + 1,)),
             dma((2,)), dma((2,)), dma((2,)), dma((2,)),
         ],
         compiler_params=pltpu.CompilerParams(
-            collective_id=0, has_side_effects=True, vmem_limit_bytes=60 * 1024 * 1024
+            collective_id=0, has_side_effects=True, vmem_limit_bytes=48 * 1024 * 1024
         ),
-    )(
-        latent, gain, conv_bias, time_bias, up_bias,
-        conv_weight, time_weight, jnp.swapaxes(up_weight, 2, 3),
-    )
+    )(*(
+        pltpu.with_memory_space_constraint(array, pltpu.HBM)
+        for array in (
+            latent, gain, conv_bias, time_bias, up_bias,
+            conv_weight, time_weight, jnp.swapaxes(up_weight, 2, 3),
+        )
+    ))
 
 
 def solution(mesh):

time: 40.3 us -> 37.5 us (0.931)
  Pallas kernels: 37.7 us -> 36 us
  local copies, waits for them, and re-layouts: 2.47 us -> 1.49 us
    pallas_call x1, Pallas kernels: 37.7 us -> 36 us  [local(): pl.pallas_call(functools.partial(kernel, frames, tiles), out_shape=jax.Sh...]
    pallas_call x1, local copies, waits for them, and re-layouts: 2.47 us -> 1.49 us  [local(): pl.pallas_call(functools.partial(kernel, frames, tiles), out_shape=jax.Sh...]
where the time goes in v4:
time: 37.5 us; the launch traced here: 37.4 us
  Pallas kernels  36 us (96%)
  local copies, waits for them, and re-layouts  1.49 us (4%)
    pallas_call x1, Pallas kernels, local(): pl.pallas_call(functools.partial(kernel, frames, tiles), out_shape=jax.Sh...  36 us
    pallas_call x1, local copies, waits for them, and re-layouts, local(): pl.pallas_call(functools.partial(kernel, frames, tiles), out_shape=jax.Sh...  1.49 us

profile of v4, /device:TPU:10, one launch (start us, length us, event | category | flops | bytes accessed | tf_op | source)
XLA Modules:
  0.0 37.4 jit_solution(3736334446681012654)
XLA Ops:
  0.0 36.0 %shard_map.82 = bf16[2,4,320,192]{3,2,1,0:T(8,128)(2,1)S(1)} custom-call(bf16[1,2,160,384]{3,2,1,0:T(8,128)(2,1)} %lat_hbm.1, f32[384]{0:T(512)} %gain_hbm.1, f32[384]{0:T(512)} %cb_hbm.1, f32[768]{0:T(1024)} %tb_hbm.1, f32[192]{0:T(256)} %ub_hbm.1, bf16[3,3,3,384,384]{4,3,2,1,0:T(8,128)(2,1)} %cw_hbm.1, bf16[3,384,768]{2,1,0:T(8,128)(2,1)} %tw_hbm.1, ...), custom_call_target="tpu_custom_call" | custom-call | tf_op jit(solution)/shard_map/pallas_call | solution.py:400
  36.0 1.5 %copy.9 = bf16[2,4,320,192]{2,3,1,0:T(8,128)(2,1)} copy(bf16[2,4,320,192]{3,2,1,0:T(8,128)(2,1)S(1)} %shard_map.82) | data formatting | bytes 1966080 | tf_op jit(solution)/shard_map/pallas_call | solution.py:400

commit v5 on v4

--- a/solution.py
+++ b/solution.py
@@ -24,10 +24,10 @@
     frames, tiles,
     lat_hbm, gain_hbm, cb_hbm, tb_hbm, ub_hbm, cw_hbm, tw_hbm, uw_hbm,
     out_ref,
-    lat, act, act_hist, parts, part_in, blk, blk_hist, dbl,
+    lat, act, act_hist, act_relay, parts, part_in, blk, blk_hist, dbl,
     gain_ref, cb_ref, tb_ref, ub_ref, cw, tw, uw, umat, acc, mixed, edge, wide_lo, wide_hi,
     lat_sem, bias_sem, cw_sem, tw_sem, uw_sem,
-    a_send, a_recv, a_fsend, b_send, b_recv, b_fsend,
+    a_send, a_recv, a_fsend, r_send, r_recv, b_send, b_recv, b_fsend,
     p_down_sem, p_up_sem, b_down_sem, d_up_sem,
 ):
     rows, cols, chans = lat.shape
@@ -69,6 +69,12 @@
     uw_copy = pltpu.make_async_copy(uw_hbm, uw, uw_sem)
     uw_copy.start()
 
+    half = frames // 2
+    partner = s + 1 - 2 * lax.rem(s, 2)
+    relays_out = t // 2 == half // 2 - 1
+    relays_in = t // 2 == half // 2
+    plain_out = jnp.logical_and(has_next, jnp.logical_not(relays_out))
+
     sibling = t + 1 - 2 * lax.rem(t, 2)
     barrier = pltpu.get_barrier_semaphore()
 
@@ -80,6 +86,8 @@
     pl.semaphore_signal(barrier, inc=1, device_id={"tm": sibling}, device_id_type=MESH)
     greet(has_next, {"tm": t + 2})
     greet(has_prev, {"tm": t - 2})
+    greet(relays_out, {"tm": t + 2, "tile": partner})
+    greet(relays_in, {"tm": t - 2, "tile": partner})
     greet(has_up, {"tile": s - 1})
     greet(has_down, {"tile": s + 1})
 
@@ -104,10 +112,10 @@
 
         return nearer, farther, forward
 
-    def history_start(copies, r):
+    def history_start(copies, r, sends=has_next):
         nearer, farther, _ = copies
 
-        @pl.when(has_next)
+        @pl.when(sends)
         def _():
             farther(r).start()
 
@@ -126,10 +134,10 @@
     def history_near(copies, r):
         copies[0](r).wait_recv()
 
-    def history_end(copies, r):
+    def history_end(copies, r, sends=has_next):
         nearer, farther, forward = copies
 
-        @pl.when(has_next)
+        @pl.when(sends)
         def _():
             farther(r).wait_send()
 
@@ -161,8 +169,20 @@
         act[r] = (scaled * jax.nn.sigmoid(scaled)).astype(BF16)
 
     peers = 1
-    for condition in (has_next, has_prev, has_up, has_down):
+    for condition in (has_next, has_prev, relays_out, relays_in, has_up, has_down):
         peers = peers + condition.astype(jnp.int32)
+
+    def relay_out(r):
+        return pltpu.make_async_remote_copy(
+            act.at[r], act_relay.at[r], r_send.at[0, r], r_recv.at[r],
+            device_id={"tm": t + 2, "tile": partner}, device_id_type=MESH,
+        )
+
+    def relay_on(r):
+        return pltpu.make_async_remote_copy(
+            act_relay.at[r], act_hist.at[0, r], r_send.at[1, r], a_recv.at[0, r],
+            device_id={"tile": partner}, device_id_type=MESH,
+        )
 
     order = tuple(range(rows))[::-1]
     lat_copy.wait()
@@ -172,7 +192,11 @@
         activate(r)
         if r == order[0]:
             pl.semaphore_wait(barrier, peers)
-        history_start(act_copies, r)
+        @pl.when(relays_out)
+        def _():
+            relay_out(r).start()
+
+        history_start(act_copies, r, plain_out)
 
     def widen(frame):
         flat = frame.reshape(-1, chans)
@@ -200,6 +224,11 @@
 
         @pl.when(has_prev)
         def _():
+            @pl.when(relays_in)
+            def _():
+                relay_out(r).wait_recv()
+                relay_on(r).start()
+
             history_far(act_copies, r)
             acc[span, :] += conv(widen(act_hist[0, r]), 0, 0, 3 * chans)
 
@@ -376,7 +405,16 @@
     upsample_row(1, last, edge[1])
 
     for r in range(rows):
-        history_end(act_copies, r)
+        history_end(act_copies, r, plain_out)
+
+        @pl.when(relays_out)
+        def _():
+            relay_out(r).wait_send()
+
+        @pl.when(relays_in)
+        def _():
+            relay_on(r).wait_send()
+
         history_end(blk_copies, 1 + r)
 
     @pl.when(has_up)
@@ -406,6 +444,7 @@
             pltpu.VMEM((rows,) + row, BF16),
             pltpu.VMEM((rows,) + row, BF16),
             pltpu.VMEM((2, rows) + row, BF16),
+            pltpu.VMEM((rows,) + row, BF16),
             pltpu.VMEM((2,) + row, BF16),
             pltpu.VMEM((2,) + row, BF16),
             pltpu.VMEM((rows + 1,) + row, BF16),
@@ -426,6 +465,7 @@
             pltpu.VMEM((2 * cols, low), F32),
             dma(()), dma((4,)), dma((3, 3)), dma(()), dma(()),
             dma((2, rows)), dma((2, rows)), dma((rows,)),
+            dma((2, rows)), dma((rows,)),
             dma((2, rows + 1)), dma((2, rows + 1)), dma((rows + 1,)),
             dma((2,)), dma((2,)), dma((2,)), dma((2,)),
         ],

time: 37.5 us -> 41.4 us (1.10)
  the two profiles are of different devices: /device:TPU:10 before, /device:TPU:52 now
where the time goes in v5:
time: 41.4 us; the launch traced here: 41.3 us
  Pallas kernels  39.8 us (96%)
  local copies, waits for them, and re-layouts  1.49 us (4%)
    pallas_call x1, Pallas kernels, local(): pl.pallas_call(functools.partial(kernel, frames, tiles), out_shape=jax.Sh...  39.8 us
    pallas_call x1, local copies, waits for them, and re-layouts, local(): pl.pallas_call(functools.partial(kernel, frames, tiles), out_shape=jax.Sh...  1.49 us

profile of v5, /device:TPU:52, one launch (start us, length us, event | category | flops | bytes accessed | tf_op | source)
XLA Modules:
  0.0 41.3 jit_solution(2728676506764943)
XLA Ops:
  0.0 39.8 %shard_map.82 = bf16[2,4,320,192]{3,2,1,0:T(8,128)(2,1)S(1)} custom-call(bf16[1,2,160,384]{3,2,1,0:T(8,128)(2,1)} %lat_hbm.1, f32[384]{0:T(512)} %gain_hbm.1, f32[384]{0:T(512)} %cb_hbm.1, f32[768]{0:T(1024)} %tb_hbm.1, f32[192]{0:T(256)} %ub_hbm.1, bf16[3,3,3,384,384]{4,3,2,1,0:T(8,128)(2,1)} %cw_hbm.1, bf16[3,384,768]{2,1,0:T(8,128)(2,1)} %tw_hbm.1, ...), custom_call_target="tpu_custom_call" | custom-call | tf_op jit(solution)/shard_map/pallas_call | solution.py:438
  39.8 1.5 %copy.9 = bf16[2,4,320,192]{2,3,1,0:T(8,128)(2,1)} copy(bf16[2,4,320,192]{3,2,1,0:T(8,128)(2,1)S(1)} %shard_map.82) | data formatting | bytes 1966080 | tf_op jit(solution)/shard_map/pallas_call | solution.py:438

commit v6 on v4

--- a/solution.py
+++ b/solution.py
@@ -24,10 +24,10 @@
     frames, tiles,
     lat_hbm, gain_hbm, cb_hbm, tb_hbm, ub_hbm, cw_hbm, tw_hbm, uw_hbm,
     out_ref,
-    lat, act, act_hist, parts, part_in, blk, blk_hist, dbl,
+    lat, act, act_hist, act_relay, parts, part_in, blk, blk_hist, dbl,
     gain_ref, cb_ref, tb_ref, ub_ref, cw, tw, uw, umat, acc, mixed, edge, wide_lo, wide_hi,
     lat_sem, bias_sem, cw_sem, tw_sem, uw_sem,
-    a_send, a_recv, a_fsend, b_send, b_recv, b_fsend,
+    a_send, a_recv, a_fsend, r_send, r_recv, b_send, b_recv, b_fsend,
     p_down_sem, p_up_sem, b_down_sem, d_up_sem,
 ):
     rows, cols, chans = lat.shape
@@ -69,6 +69,12 @@
     uw_copy = pltpu.make_async_copy(uw_hbm, uw, uw_sem)
     uw_copy.start()
 
+    half = frames // 2
+    partner = s + 1 - 2 * lax.rem(s, 2)
+    relays = t // 2 == half // 2 - 1
+    relayed = t // 2 == half // 2
+    direct = jnp.logical_and(has_next, jnp.logical_not(relays))
+
     sibling = t + 1 - 2 * lax.rem(t, 2)
     barrier = pltpu.get_barrier_semaphore()
 
@@ -80,6 +86,8 @@
     pl.semaphore_signal(barrier, inc=1, device_id={"tm": sibling}, device_id_type=MESH)
     greet(has_next, {"tm": t + 2})
     greet(has_prev, {"tm": t - 2})
+    greet(relays, {"tm": t + 2, "tile": partner})
+    greet(relayed, {"tm": t - 2, "tile": partner})
     greet(has_up, {"tile": s - 1})
     greet(has_down, {"tile": s + 1})
 
@@ -104,10 +112,10 @@
 
         return nearer, farther, forward
 
-    def history_start(copies, r):
+    def history_start(copies, r, sends=has_next):
         nearer, farther, _ = copies
 
-        @pl.when(has_next)
+        @pl.when(sends)
         def _():
             farther(r).start()
 
@@ -126,10 +134,10 @@
     def history_near(copies, r):
         copies[0](r).wait_recv()
 
-    def history_end(copies, r):
+    def history_end(copies, r, sends=has_next):
         nearer, farther, forward = copies
 
-        @pl.when(has_next)
+        @pl.when(sends)
         def _():
             farther(r).wait_send()
 
@@ -161,8 +169,20 @@
         act[r] = (scaled * jax.nn.sigmoid(scaled)).astype(BF16)
 
     peers = 1
-    for condition in (has_next, has_prev, has_up, has_down):
+    for condition in (has_next, has_prev, relays, relayed, has_up, has_down):
         peers = peers + condition.astype(jnp.int32)
+
+    def to_partner(r):
+        return pltpu.make_async_remote_copy(
+            act.at[r], act_relay.at[r], r_send.at[0, r], r_recv.at[r],
+            device_id={"tile": partner}, device_id_type=MESH,
+        )
+
+    def from_partner(r):
+        return pltpu.make_async_remote_copy(
+            act_relay.at[r], act_hist.at[0, r], r_send.at[1, r], a_recv.at[0, r],
+            device_id={"tm": t + 2, "tile": partner}, device_id_type=MESH,
+        )
 
     order = tuple(range(rows))[::-1]
     lat_copy.wait()
@@ -172,7 +192,14 @@
         activate(r)
         if r == order[0]:
             pl.semaphore_wait(barrier, peers)
-        history_start(act_copies, r)
+        if r == order[0]:
+            history_start(act_copies, r)
+        else:
+            @pl.when(relays)
+            def _():
+                to_partner(r).start()
+
+            history_start(act_copies, r, direct)
 
     def widen(frame):
         flat = frame.reshape(-1, chans)
@@ -193,6 +220,13 @@
     acc[...] = conv(widen(act[...]), 2, 0, 3 * chans)
     weights_ready(0)
     weights_ready(1)
+
+    @pl.when(relays)
+    def _():
+        for r in order[1:]:
+            to_partner(r).wait_recv()
+            from_partner(r).start()
+
     for r in order:
         span = pl.ds(r * cols, cols)
         goes, stays = (0, chans) if r == last else (2 * chans, 0)
@@ -348,8 +382,8 @@
             wide_lo[pl.ds(1, cols, stride=2), :] = uneven[span]
             wide_hi[pl.ds(0, cols, stride=2), :] = tail[span]
             wide_hi[pl.ds(1, cols, stride=2), :] = swapped[span]
-            out_ref[f, 2 * r + a, :, pl.ds(0, low)] = wide_lo[...].astype(BF16)
-            out_ref[f, 2 * r + a, :, pl.ds(low, high)] = wide_hi[:, :high].astype(BF16)
+            out_ref[f, 2 * r + a, pl.ds(0, low), :] = wide_lo[...].T.astype(BF16)
+            out_ref[f, 2 * r + a, pl.ds(low, high), :] = wide_hi[...].T[:high].astype(BF16)
 
     for r in range(rows):
         for a in range(2):
@@ -376,8 +410,14 @@
     upsample_row(1, last, edge[1])
 
     for r in range(rows):
-        history_end(act_copies, r)
+        history_end(act_copies, r, has_next if r == order[0] else direct)
         history_end(blk_copies, 1 + r)
+
+    @pl.when(relays)
+    def _():
+        for r in order[1:]:
+            to_partner(r).wait_send()
+            from_partner(r).wait_send()
 
     @pl.when(has_up)
     def _():
@@ -397,15 +437,16 @@
     low = 128
     dma = pltpu.SemaphoreType.DMA
     row = (cols, chans)
-    return pl.pallas_call(
+    transposed = pl.pallas_call(
         functools.partial(kernel, frames, tiles),
-        out_shape=jax.ShapeDtypeStruct((2, 2 * rows, 2 * cols, outs_n), BF16),
+        out_shape=jax.ShapeDtypeStruct((2, 2 * rows, outs_n, 2 * cols), BF16),
         in_specs=[pl.BlockSpec(memory_space=pltpu.HBM)] * 8,
         out_specs=pl.BlockSpec(memory_space=pltpu.VMEM),
         scratch_shapes=[
             pltpu.VMEM((rows,) + row, BF16),
             pltpu.VMEM((rows,) + row, BF16),
             pltpu.VMEM((2, rows) + row, BF16),
+            pltpu.VMEM((rows,) + row, BF16),
             pltpu.VMEM((2,) + row, BF16),
             pltpu.VMEM((2,) + row, BF16),
             pltpu.VMEM((rows + 1,) + row, BF16),
@@ -426,6 +467,7 @@
             pltpu.VMEM((2 * cols, low), F32),
             dma(()), dma((4,)), dma((3, 3)), dma(()), dma(()),
             dma((2, rows)), dma((2, rows)), dma((rows,)),
+            dma((2, rows)), dma((rows,)),
             dma((2, rows + 1)), dma((2, rows + 1)), dma((rows + 1,)),
             dma((2,)), dma((2,)), dma((2,)), dma((2,)),
         ],
@@ -439,6 +481,7 @@
             conv_weight, time_weight, jnp.swapaxes(up_weight, 2, 3),
         )
     ))
+    return jnp.swapaxes(transposed, 2, 3)
 
 
 def solution(mesh):

time: 37.5 us -> 35.7 us (0.952)
  the two profiles are of different devices: /device:TPU:10 before, /device:TPU:1 now
where the time goes in v6:
time: 35.7 us
  Pallas kernels  34.6 us (97%)
  local copies, waits for them, and re-layouts  1.02 us (3%)
    pallas_call x1, Pallas kernels, local(): pl.pallas_call(functools.partial(kernel, frames, tiles), out_shape=jax.Sh...  34.6 us
    unnamed x1, local copies, waits for them, and re-layouts  1.02 us

profile of v6, /device:TPU:1, one launch (start us, length us, event | category | flops | bytes accessed | tf_op | source)
XLA Modules:
  0.0 35.7 jit_solution(3771163311314132527)
XLA Ops:
  0.0 34.6 %shard_map.82 = bf16[2,4,192,320]{3,2,1,0:T(8,128)(2,1)S(1)} custom-call(bf16[1,2,160,384]{3,2,1,0:T(8,128)(2,1)} %lat_hbm.1, f32[384]{0:T(512)} %gain_hbm.1, f32[384]{0:T(512)} %cb_hbm.1, f32[768]{0:T(1024)} %tb_hbm.1, f32[192]{0:T(256)} %ub_hbm.1, bf16[3,3,3,384,384]{4,3,2,1,0:T(8,128)(2,1)} %cw_hbm.1, bf16[3,384,768]{2,1,0:T(8,128)(2,1)} %tw_hbm.1, ...), custom_call_target="tpu_custom_call" | custom-call | tf_op jit(solution)/shard_map/pallas_call | solution.py:440
  34.6 1.0 %copy.10 = bf16[2,4,320,192]{2,3,1,0:T(8,128)(2,1)} copy(bf16[2,4,320,192]{2,3,1,0:T(8,128)(2,1)S(1)} %bitcast.2) | data formatting | bytes 1966080

commit v7 on v6

--- a/solution.py
+++ b/solution.py
@@ -35,6 +35,8 @@
     low = 128
     high = outs_n - low
     cells = rows * cols
+    middle = cols // 2
+    margin = 16
     t = lax.axis_index("tm")
     s = lax.axis_index("tile")
     odd = lax.rem(t, 2) == 1
@@ -91,22 +93,27 @@
     greet(has_up, {"tile": s - 1})
     greet(has_down, {"tile": s + 1})
 
-    def history_copies(own, hist, send, recv, fsend):
-        def nearer(r):
+    def piece(k):
+        r, right = divmod(k, 2)
+        start, size = (middle + margin, middle - margin) if right else (0, middle + margin)
+        return (r, pl.ds(start, size))
+
+    def history_copies(own, hist, send, recv, fsend, at=lambda k: (k,)):
+        def nearer(k):
             return pltpu.make_async_remote_copy(
-                own.at[r], hist.at[1, r], send.at[0, r], recv.at[1, r],
+                own.at[at(k)], hist.at[(1,) + at(k)], send.at[0, k], recv.at[1, k],
                 device_id={"tm": sibling}, device_id_type=MESH,
             )
 
-        def farther(r):
+        def farther(k):
             return pltpu.make_async_remote_copy(
-                own.at[r], hist.at[0, r], send.at[1, r], recv.at[0, r],
+                own.at[at(k)], hist.at[(0,) + at(k)], send.at[1, k], recv.at[0, k],
                 device_id={"tm": t + 2}, device_id_type=MESH,
             )
 
-        def forward(r):
+        def forward(k):
             return pltpu.make_async_remote_copy(
-                hist.at[0, r], hist.at[1, r], fsend.at[r], recv.at[1, r],
+                hist.at[(0,) + at(k)], hist.at[(1,) + at(k)], fsend.at[k], recv.at[1, k],
                 device_id={"tm": sibling}, device_id_type=MESH,
             )
 
@@ -155,10 +162,15 @@
         )
 
     first, last = 0, rows - 1
-    act_copies = history_copies(act, act_hist, a_send, a_recv, a_fsend)
+    act_copies = history_copies(act, act_hist, a_send, a_recv, a_fsend, piece)
     blk_copies = history_copies(blk, blk_hist, b_send, b_recv, b_fsend)
-    part_down = to_tile(parts.at[1], part_in.at[0], p_down_sem, s + 1)
-    part_up = to_tile(parts.at[0], part_in.at[1], p_up_sem, s - 1)
+    half_row = [pl.ds(0, middle), pl.ds(middle, middle)]
+    part_down = [
+        to_tile(parts.at[1, w], part_in.at[0, w], p_down_sem.at[h], s + 1) for h, w in enumerate(half_row)
+    ]
+    part_up = [
+        to_tile(parts.at[0, w], part_in.at[1, w], p_up_sem.at[h], s - 1) for h, w in enumerate(half_row)
+    ]
     blk_down = to_tile(blk.at[rows], blk.at[0], b_down_sem, s + 1)
     dbl_up = to_tile(dbl.at[1], dbl.at[rows + 1], d_up_sem, s - 1)
 
@@ -172,41 +184,50 @@
     for condition in (has_next, has_prev, relays, relayed, has_up, has_down):
         peers = peers + condition.astype(jnp.int32)
 
-    def to_partner(r):
+    def to_partner(k):
         return pltpu.make_async_remote_copy(
-            act.at[r], act_relay.at[r], r_send.at[0, r], r_recv.at[r],
+            act.at[piece(k)], act_relay.at[piece(k)], r_send.at[0, k], r_recv.at[k],
             device_id={"tile": partner}, device_id_type=MESH,
         )
 
-    def from_partner(r):
+    def from_partner(k):
         return pltpu.make_async_remote_copy(
-            act_relay.at[r], act_hist.at[0, r], r_send.at[1, r], a_recv.at[0, r],
+            act_relay.at[piece(k)], act_hist.at[(0,) + piece(k)], r_send.at[1, k], a_recv.at[0, k],
             device_id={"tm": t + 2, "tile": partner}, device_id_type=MESH,
         )
 
     order = tuple(range(rows))[::-1]
+    near_pieces = (2 * last, 2 * last + 1)
+    relay_pieces = tuple(2 * r + h for r in order[1:] for h in range(2))
     lat_copy.wait()
     for copy in bias_copies:
         copy.wait()
     for r in order:
         activate(r)
-        if r == order[0]:
+        if r == last:
             pl.semaphore_wait(barrier, peers)
-        if r == order[0]:
-            history_start(act_copies, r)
+            for k in near_pieces:
+                history_start(act_copies, k)
         else:
-            @pl.when(relays)
-            def _():
-                to_partner(r).start()
-
-            history_start(act_copies, r, direct)
-
-    def widen(frame):
-        flat = frame.reshape(-1, chans)
+            for k in (2 * r, 2 * r + 1):
+                @pl.when(relays)
+                def _():
+                    to_partner(k).start()
+
+                history_start(act_copies, k, direct)
+
+    def widen(flat):
         wide = flat.astype(F32)
-        before = column_shift(wide, cols, 1).astype(BF16)
-        after = column_shift(wide, cols, -1).astype(BF16)
+        size = flat.shape[0]
+        run = min(size, cols)
+        before = column_shift(wide, run, 1).astype(BF16)
+        after = column_shift(wide, run, -1).astype(BF16)
         return jnp.concatenate([before, flat, after], axis=1)
+
+    def widen_half(slot, r, h):
+        if h == 0:
+            return widen(act_hist[slot, r, pl.ds(0, middle + margin)])[:middle]
+        return widen(act_hist[slot, r, pl.ds(middle - margin, middle + margin)])[margin:]
 
     def conv(stacked, dt, start, size):
         taps = cw.at[dt, :, :, pl.ds(start, size)][...].reshape(3 * chans, size)
@@ -217,85 +238,13 @@
             cw_copies[dt, dh].wait()
 
     weights_ready(2)
-    acc[...] = conv(widen(act[...]), 2, 0, 3 * chans)
-    weights_ready(0)
-    weights_ready(1)
+    acc[...] = conv(widen(act[...].reshape(cells, chans)), 2, 0, 3 * chans)
 
     @pl.when(relays)
     def _():
-        for r in order[1:]:
-            to_partner(r).wait_recv()
-            from_partner(r).start()
-
-    for r in order:
-        span = pl.ds(r * cols, cols)
-        goes, stays = (0, chans) if r == last else (2 * chans, 0)
-        out_part = 1 if r == last else 0
-
-        @pl.when(has_prev)
-        def _():
-            history_far(act_copies, r)
-            acc[span, :] += conv(widen(act_hist[0, r]), 0, 0, 3 * chans)
-
-        @pl.when(has_near)
-        def _():
-            history_near(act_copies, r)
-            acc[span, pl.ds(goes, chans)] += conv(widen(act_hist[1, r]), 1, goes, chans)
-
-        parts[out_part] = acc[span, pl.ds(goes, chans)].astype(BF16)
-        if r == last:
-            @pl.when(has_down)
-            def _():
-                part_down.start()
-        else:
-            @pl.when(has_up)
-            def _():
-                part_up.start()
-
-        @pl.when(has_near)
-        def _():
-            acc[span, pl.ds(stays, 2 * chans)] += conv(widen(act_hist[1, r]), 1, stays, 2 * chans)
-
-    def finish_row(r):
-        total = acc[pl.ds(r * cols, cols), pl.ds(chans, chans)]
-        if r > 0:
-            total = total + acc[pl.ds((r - 1) * cols, cols), pl.ds(0, chans)]
-        if r < rows - 1:
-            total = total + acc[pl.ds((r + 1) * cols, cols), pl.ds(2 * chans, chans)]
-        total = total + cb_ref[...].reshape(1, chans) + lat[r].astype(F32)
-        if r == first:
-            total = total + part_in[0].astype(F32)
-        if r == last:
-            total = total + part_in[1].astype(F32)
-        blk[1 + r] = total.astype(BF16)
-
-    @pl.when(has_up)
-    def _():
-        part_down.wait_recv()
-
-    @pl.when(jnp.logical_not(has_up))
-    def _():
-        part_in[0] = jnp.zeros((cols, chans), BF16)
-
-    for r in range(rows - 1):
-        finish_row(r)
-        history_start(blk_copies, 1 + r)
-
-    @pl.when(has_down)
-    def _():
-        part_up.wait_recv()
-
-    @pl.when(jnp.logical_not(has_down))
-    def _():
-        part_in[1] = jnp.zeros((cols, chans), BF16)
-
-    finish_row(last)
-
-    @pl.when(has_down)
-    def _():
-        blk_down.start()
-
-    history_start(blk_copies, rows)
+        for k in relay_pieces:
+            to_partner(k).wait_recv()
+            from_partner(k).start()
 
     uw_copy.wait()
     row_sets = {(0, 0): (0,), (0, 1): (1, 2), (1, 0): (0, 1), (1, 1): (2,)}
@@ -315,6 +264,52 @@
                 umat[a, pl.ds(base + b * low, low), lanes] = value[:low]
                 umat[a, pl.ds(base + 2 * low + b * high, high), lanes] = value[low:]
 
+    weights_ready(0)
+    weights_ready(1)
+    for r in order:
+        goes, stays = (0, chans) if r == last else (2 * chans, 0)
+        out_part = 1 if r == last else 0
+        for h in range(2):
+            k = 2 * r + h
+            span = pl.ds(r * cols + h * middle, middle)
+
+            @pl.when(has_prev)
+            def _():
+                history_far(act_copies, k)
+                acc[span, :] += conv(widen_half(0, r, h), 0, 0, 3 * chans)
+
+            @pl.when(has_near)
+            def _():
+                history_near(act_copies, k)
+                acc[span, pl.ds(goes, chans)] += conv(widen_half(1, r, h), 1, goes, chans)
+
+            parts[out_part, half_row[h]] = acc[span, pl.ds(goes, chans)].astype(BF16)
+            if r == last:
+                @pl.when(has_down)
+                def _():
+                    part_down[h].start()
+            else:
+                @pl.when(has_up)
+                def _():
+                    part_up[h].start()
+
+            @pl.when(has_near)
+            def _():
+                acc[span, pl.ds(stays, 2 * chans)] += conv(widen_half(1, r, h), 1, stays, 2 * chans)
+
+    def finish_row(r):
+        total = acc[pl.ds(r * cols, cols), pl.ds(chans, chans)]
+        if r > 0:
+            total = total + acc[pl.ds((r - 1) * cols, cols), pl.ds(0, chans)]
+        if r < rows - 1:
+            total = total + acc[pl.ds((r + 1) * cols, cols), pl.ds(2 * chans, chans)]
+        total = total + cb_ref[...].reshape(1, chans) + lat[r].astype(F32)
+        if r == first:
+            total = total + part_in[0].astype(F32)
+        if r == last:
+            total = total + part_in[1].astype(F32)
+        blk[1 + r] = total.astype(BF16)
+
     tw_copy.wait()
 
     def mix(row, k):
@@ -337,8 +332,38 @@
         for f in range(2):
             dbl[j, f] = mixed[j, :, pl.ds(f * chans, chans)].astype(BF16)
 
-    for r in range(rows):
+    @pl.when(has_up)
+    def _():
+        for copy in part_down:
+            copy.wait_recv()
+
+    @pl.when(jnp.logical_not(has_up))
+    def _():
+        part_in[0] = jnp.zeros((cols, chans), BF16)
+
+    for r in range(rows - 1):
+        finish_row(r)
+        history_start(blk_copies, 1 + r)
         newest(1 + r)
+
+    @pl.when(has_down)
+    def _():
+        for copy in part_up:
+            copy.wait_recv()
+
+    @pl.when(jnp.logical_not(has_down))
+    def _():
+        part_in[1] = jnp.zeros((cols, chans), BF16)
+
+    finish_row(last)
+
+    @pl.when(has_down)
+    def _():
+        blk_down.start()
+
+    history_start(blk_copies, rows)
+    newest(rows)
+
     for r in range(rows):
         if r == last:
             @pl.when(has_up)
@@ -410,24 +435,27 @@
     upsample_row(1, last, edge[1])
 
     for r in range(rows):
-        history_end(act_copies, r, has_next if r == order[0] else direct)
+        for k in (2 * r, 2 * r + 1):
+            history_end(act_copies, k, has_next if k in near_pieces else direct)
         history_end(blk_copies, 1 + r)
 
     @pl.when(relays)
     def _():
-        for r in order[1:]:
-            to_partner(r).wait_send()
-            from_partner(r).wait_send()
+        for k in relay_pieces:
+            to_partner(k).wait_send()
+            from_partner(k).wait_send()
 
     @pl.when(has_up)
     def _():
         history_end(blk_copies, 0)
-        part_up.wait_send()
+        for copy in part_up:
+            copy.wait_send()
         dbl_up.wait_send()
 
     @pl.when(has_down)
     def _():
-        part_down.wait_send()
+        for copy in part_down:
+            copy.wait_send()
         blk_down.wait_send()
 
 
@@ -466,10 +494,10 @@
             pltpu.VMEM((2 * cols, low), F32),
             pltpu.VMEM((2 * cols, low), F32),
             dma(()), dma((4,)), dma((3, 3)), dma(()), dma(()),
-            dma((2, rows)), dma((2, rows)), dma((rows,)),
-            dma((2, rows)), dma((rows,)),
+            dma((2, 2 * rows)), dma((2, 2 * rows)), dma((2 * rows,)),
+            dma((2, 2 * rows)), dma((2 * rows,)),
             dma((2, rows + 1)), dma((2, rows + 1)), dma((rows + 1,)),
-            dma((2,)), dma((2,)), dma((2,)), dma((2,)),
+            dma((2, 2)), dma((2, 2)), dma((2,)), dma((2,)),
         ],
         compiler_params=pltpu.CompilerParams(
             collective_id=0, has_side_effects=True, vmem_limit_bytes=48 * 1024 * 1024

time: 35.7 us -> 36 us (level)
  the two profiles are of different devices: /device:TPU:1 before, /device:TPU:28 now
where the time goes in v7:
time: 36 us; the launch traced here: 35.4 us
  Pallas kernels  34.3 us (95%)
  local copies, waits for them, and re-layouts  1.02 us (3%)
    pallas_call x1, Pallas kernels, local(): pl.pallas_call(functools.partial(kernel, frames, tiles), out_shape=jax.Sh...  34.3 us
    unnamed x1, local copies, waits for them, and re-layouts  1.02 us

profile of v7, /device:TPU:28, one launch (start us, length us, event | category | flops | bytes accessed | tf_op | source)
XLA Modules:
  0.0 35.4 jit_solution(11533695558062452856)
XLA Ops:
  0.0 34.3 %shard_map.82 = bf16[2,4,192,320]{3,2,1,0:T(8,128)(2,1)S(1)} custom-call(bf16[1,2,160,384]{3,2,1,0:T(8,128)(2,1)} %lat_hbm.1, f32[384]{0:T(512)} %gain_hbm.1, f32[384]{0:T(512)} %cb_hbm.1, f32[768]{0:T(1024)} %tb_hbm.1, f32[192]{0:T(256)} %ub_hbm.1, bf16[3,3,3,384,384]{4,3,2,1,0:T(8,128)(2,1)} %cw_hbm.1, bf16[3,384,768]{2,1,0:T(8,128)(2,1)} %tw_hbm.1, ...), custom_call_target="tpu_custom_call" | custom-call | tf_op jit(solution)/shard_map/pallas_call | solution.py:468
  34.4 1.0 %copy.10 = bf16[2,4,320,192]{2,3,1,0:T(8,128)(2,1)} copy(bf16[2,4,320,192]{2,3,1,0:T(8,128)(2,1)S(1)} %bitcast.2) | data formatting | bytes 1966080

commit v8 on v6

--- a/solution.py
+++ b/solution.py
@@ -24,11 +24,11 @@
     frames, tiles,
     lat_hbm, gain_hbm, cb_hbm, tb_hbm, ub_hbm, cw_hbm, tw_hbm, uw_hbm,
     out_ref,
-    lat, act, act_hist, act_relay, parts, part_in, blk, blk_hist, dbl,
+    lat, act, act_hist, act_relay, parts, part_in, blk, blk_hist, blk_relay, dbl,
     gain_ref, cb_ref, tb_ref, ub_ref, cw, tw, uw, umat, acc, mixed, edge, wide_lo, wide_hi,
     lat_sem, bias_sem, cw_sem, tw_sem, uw_sem,
     a_send, a_recv, a_fsend, r_send, r_recv, b_send, b_recv, b_fsend,
-    p_down_sem, p_up_sem, b_down_sem, d_up_sem,
+    p_down_sem, p_up_sem, b_down_sem, b_up_sem, d_up_sem, q_sem,
 ):
     rows, cols, chans = lat.shape
     outs_n = uw.shape[2]
@@ -42,6 +42,8 @@
     has_next = t + 2 < frames
     has_prev = t >= 2
     has_near = t >= 1
+    starts = t < 2
+    later = t >= 2
     has_up = s > 0
     has_down = s < tiles - 1
 
@@ -160,6 +162,7 @@
     part_down = to_tile(parts.at[1], part_in.at[0], p_down_sem, s + 1)
     part_up = to_tile(parts.at[0], part_in.at[1], p_up_sem, s - 1)
     blk_down = to_tile(blk.at[rows], blk.at[0], b_down_sem, s + 1)
+    blk_up = to_tile(blk.at[1], blk.at[rows + 1], b_up_sem, s - 1)
     dbl_up = to_tile(dbl.at[1], dbl.at[rows + 1], d_up_sem, s - 1)
 
     def activate(r):
@@ -183,6 +186,14 @@
             act_relay.at[r], act_hist.at[0, r], r_send.at[1, r], a_recv.at[0, r],
             device_id={"tm": t + 2, "tile": partner}, device_id_type=MESH,
         )
+
+    blk_to_partner = pltpu.make_async_remote_copy(
+        blk.at[rows], blk_relay, q_sem.at[0], q_sem.at[1], device_id={"tile": partner}, device_id_type=MESH
+    )
+    blk_from_partner = pltpu.make_async_remote_copy(
+        blk_relay, blk_hist.at[0, rows], q_sem.at[2], b_recv.at[0, rows],
+        device_id={"tm": t + 2, "tile": partner}, device_id_type=MESH,
+    )
 
     order = tuple(range(rows))[::-1]
     lat_copy.wait()
@@ -218,84 +229,11 @@
 
     weights_ready(2)
     acc[...] = conv(widen(act[...]), 2, 0, 3 * chans)
-    weights_ready(0)
-    weights_ready(1)
-
     @pl.when(relays)
     def _():
         for r in order[1:]:
             to_partner(r).wait_recv()
             from_partner(r).start()
-
-    for r in order:
-        span = pl.ds(r * cols, cols)
-        goes, stays = (0, chans) if r == last else (2 * chans, 0)
-        out_part = 1 if r == last else 0
-
-        @pl.when(has_prev)
-        def _():
-            history_far(act_copies, r)
-            acc[span, :] += conv(widen(act_hist[0, r]), 0, 0, 3 * chans)
-
-        @pl.when(has_near)
-        def _():
-            history_near(act_copies, r)
-            acc[span, pl.ds(goes, chans)] += conv(widen(act_hist[1, r]), 1, goes, chans)
-
-        parts[out_part] = acc[span, pl.ds(goes, chans)].astype(BF16)
-        if r == last:
-            @pl.when(has_down)
-            def _():
-                part_down.start()
-        else:
-            @pl.when(has_up)
-            def _():
-                part_up.start()
-
-        @pl.when(has_near)
-        def _():
-            acc[span, pl.ds(stays, 2 * chans)] += conv(widen(act_hist[1, r]), 1, stays, 2 * chans)
-
-    def finish_row(r):
-        total = acc[pl.ds(r * cols, cols), pl.ds(chans, chans)]
-        if r > 0:
-            total = total + acc[pl.ds((r - 1) * cols, cols), pl.ds(0, chans)]
-        if r < rows - 1:
-            total = total + acc[pl.ds((r + 1) * cols, cols), pl.ds(2 * chans, chans)]
-        total = total + cb_ref[...].reshape(1, chans) + lat[r].astype(F32)
-        if r == first:
-            total = total + part_in[0].astype(F32)
-        if r == last:
-            total = total + part_in[1].astype(F32)
-        blk[1 + r] = total.astype(BF16)
-
-    @pl.when(has_up)
-    def _():
-        part_down.wait_recv()
-
-    @pl.when(jnp.logical_not(has_up))
-    def _():
-        part_in[0] = jnp.zeros((cols, chans), BF16)
-
-    for r in range(rows - 1):
-        finish_row(r)
-        history_start(blk_copies, 1 + r)
-
-    @pl.when(has_down)
-    def _():
-        part_up.wait_recv()
-
-    @pl.when(jnp.logical_not(has_down))
-    def _():
-        part_in[1] = jnp.zeros((cols, chans), BF16)
-
-    finish_row(last)
-
-    @pl.when(has_down)
-    def _():
-        blk_down.start()
-
-    history_start(blk_copies, rows)
 
     uw_copy.wait()
     row_sets = {(0, 0): (0,), (0, 1): (1, 2), (1, 0): (0, 1), (1, 1): (2,)}
@@ -315,6 +253,50 @@
                 umat[a, pl.ds(base + b * low, low), lanes] = value[:low]
                 umat[a, pl.ds(base + 2 * low + b * high, high), lanes] = value[low:]
 
+    weights_ready(0)
+    weights_ready(1)
+    for r in order:
+        span = pl.ds(r * cols, cols)
+        goes, stays = (0, chans) if r == last else (2 * chans, 0)
+        out_part = 1 if r == last else 0
+
+        @pl.when(has_prev)
+        def _():
+            history_far(act_copies, r)
+            acc[span, :] += conv(widen(act_hist[0, r]), 0, 0, 3 * chans)
+
+        @pl.when(has_near)
+        def _():
+            history_near(act_copies, r)
+            acc[span, pl.ds(goes, chans)] += conv(widen(act_hist[1, r]), 1, goes, chans)
+
+        parts[out_part] = acc[span, pl.ds(goes, chans)].astype(BF16)
+        if r == last:
+            @pl.when(has_down)
+            def _():
+                part_down.start()
+        else:
+            @pl.when(has_up)
+            def _():
+                part_up.start()
+
+        @pl.when(has_near)
+        def _():
+            acc[span, pl.ds(stays, 2 * chans)] += conv(widen(act_hist[1, r]), 1, stays, 2 * chans)
+
+    def finish_row(r):
+        total = acc[pl.ds(r * cols, cols), pl.ds(chans, chans)]
+        if r > 0:
+            total = total + acc[pl.ds((r - 1) * cols, cols), pl.ds(0, chans)]
+        if r < rows - 1:
+            total = total + acc[pl.ds((r + 1) * cols, cols), pl.ds(2 * chans, chans)]
+        total = total + cb_ref[...].reshape(1, chans) + lat[r].astype(F32)
+        if r == first:
+            total = total + part_in[0].astype(F32)
+        if r == last:
+            total = total + part_in[1].astype(F32)
+        blk[1 + r] = total.astype(BF16)
+
     tw_copy.wait()
 
     def mix(row, k):
@@ -337,10 +319,53 @@
         for f in range(2):
             dbl[j, f] = mixed[j, :, pl.ds(f * chans, chans)].astype(BF16)
 
-    for r in range(rows):
+    @pl.when(has_up)
+    def _():
+        part_down.wait_recv()
+
+    @pl.when(jnp.logical_not(has_up))
+    def _():
+        part_in[0] = jnp.zeros((cols, chans), BF16)
+
+    for r in range(rows - 1):
+        finish_row(r)
+
+        if r == first:
+            @pl.when(has_up & starts)
+            def _():
+                blk_up.start()
+
+        history_start(blk_copies, 1 + r)
         newest(1 + r)
+
+    @pl.when(has_down)
+    def _():
+        part_up.wait_recv()
+
+    @pl.when(jnp.logical_not(has_down))
+    def _():
+        part_in[1] = jnp.zeros((cols, chans), BF16)
+
+    finish_row(last)
+
+    @pl.when(has_down)
+    def _():
+        blk_down.start()
+
+    @pl.when(relays)
+    def _():
+        blk_to_partner.start()
+
+    history_start(blk_copies, rows, direct)
+    newest(rows)
+
     for r in range(rows):
         if r == last:
+            @pl.when(relays)
+            def _():
+                blk_to_partner.wait_recv()
+                blk_from_partner.start()
+
             @pl.when(has_up)
             def _():
                 blk_down.wait_recv()
@@ -348,9 +373,14 @@
 
         mix_row(1 + r)
         if r == first:
-            @pl.when(has_up)
+            @pl.when(has_up & later)
             def _():
                 dbl_up.start()
+
+            @pl.when(has_down & (t == 0))
+            def _():
+                blk_up.wait_recv()
+                blk_copies[0](rows + 1).start()
 
     bias_row = ub_ref[...].reshape(1, outs_n)
     up_bias = jnp.concatenate(
@@ -402,33 +432,65 @@
 
     upsample_row(0, 0, edge[0])
 
+    @pl.when(has_down & starts)
+    def _():
+        @pl.when(t == 1)
+        def _():
+            blk_up.wait_recv()
+
+        newest(rows + 1)
+
+        @pl.when(t == 1)
+        def _():
+            history_near(blk_copies, rows + 1)
+            mixed[rows + 1] += mix(blk_hist[1, rows + 1], 1)
+
+        for f in range(2):
+            dbl[rows + 1, f] = mixed[rows + 1, :, pl.ds(f * chans, chans)].astype(BF16)
+
+    @pl.when(has_down & later)
+    def _():
+        dbl_up.wait_recv()
+
     @pl.when(has_down)
     def _():
-        dbl_up.wait_recv()
         edge[1] += taps_dot(stored_row(rows + 1), 1, chans, chans)
 
     upsample_row(1, last, edge[1])
 
     for r in range(rows):
         history_end(act_copies, r, has_next if r == order[0] else direct)
-        history_end(blk_copies, 1 + r)
+        history_end(blk_copies, 1 + r, direct if r == last else has_next)
 
     @pl.when(relays)
     def _():
         for r in order[1:]:
             to_partner(r).wait_send()
             from_partner(r).wait_send()
+        blk_to_partner.wait_send()
+        blk_from_partner.wait_send()
 
     @pl.when(has_up)
     def _():
         history_end(blk_copies, 0)
         part_up.wait_send()
-        dbl_up.wait_send()
+
+        @pl.when(later)
+        def _():
+            dbl_up.wait_send()
+
+        @pl.when(starts)
+        def _():
+            blk_up.wait_send()
 
     @pl.when(has_down)
     def _():
         part_down.wait_send()
         blk_down.wait_send()
+
+        @pl.when(t == 0)
+        def _():
+            blk_copies[0](rows + 1).wait_send()
 
 
 def local(frames, tiles, latent, gain, conv_weight, conv_bias, time_weight, time_bias, up_weight, up_bias):
@@ -449,8 +511,9 @@
             pltpu.VMEM((rows,) + row, BF16),
             pltpu.VMEM((2,) + row, BF16),
             pltpu.VMEM((2,) + row, BF16),
-            pltpu.VMEM((rows + 1,) + row, BF16),
-            pltpu.VMEM((2, rows + 1) + row, BF16),
+            pltpu.VMEM((rows + 2,) + row, BF16),
+            pltpu.VMEM((2, rows + 2) + row, BF16),
+            pltpu.VMEM(row, BF16),
             pltpu.VMEM((rows + 2, 2) + row, BF16),
             pltpu.VMEM((chans,), F32),
             pltpu.VMEM((chans,), F32),
@@ -461,15 +524,15 @@
             pltpu.VMEM((3, 3, outs_n, chans), BF16),
             pltpu.VMEM((2, 4 * outs_n, 2 * chans), BF16),
             pltpu.VMEM((rows * cols, 3 * chans), F32),
-            pltpu.VMEM((rows + 1, cols, 2 * chans), F32),
+            pltpu.VMEM((rows + 2, cols, 2 * chans), F32),
             pltpu.VMEM((2, 2 * cols, 4 * outs_n), F32),
             pltpu.VMEM((2 * cols, low), F32),
             pltpu.VMEM((2 * cols, low), F32),
             dma(()), dma((4,)), dma((3, 3)), dma(()), dma(()),
             dma((2, rows)), dma((2, rows)), dma((rows,)),
             dma((2, rows)), dma((rows,)),
-            dma((2, rows + 1)), dma((2, rows + 1)), dma((rows + 1,)),
-            dma((2,)), dma((2,)), dma((2,)), dma((2,)),
+            dma((2, rows + 2)), dma((2, rows + 2)), dma((rows + 2,)),
+            dma((2,)), dma((2,)), dma((2,)), dma((2,)), dma((2,)), dma((3,)),
         ],
         compiler_params=pltpu.CompilerParams(
             collective_id=0, has_side_effects=True, vmem_limit_bytes=48 * 1024 * 1024

time: 35.7 us -> 41.1 us (1.15)
  the two profiles are of different devices: /device:TPU:1 before, /device:TPU:6 now
where the time goes in v8:
time: 41.1 us; the launch traced here: 41 us
  Pallas kernels  40 us (97%)
  local copies, waits for them, and re-layouts  1.02 us (2%)
    pallas_call x1, Pallas kernels, local(): pl.pallas_call(functools.partial(kernel, frames, tiles), out_shape=jax.Sh...  40 us
    unnamed x1, local copies, waits for them, and re-layouts  1.02 us

profile of v8, /device:TPU:6, one launch (start us, length us, event | category | flops | bytes accessed | tf_op | source)
XLA Modules:
  0.0 41.0 jit_solution(254962451207851834)
XLA Ops:
  0.0 40.0 %shard_map.82 = bf16[2,4,192,320]{3,2,1,0:T(8,128)(2,1)S(1)} custom-call(bf16[1,2,160,384]{3,2,1,0:T(8,128)(2,1)} %lat_hbm.1, f32[384]{0:T(512)} %gain_hbm.1, f32[384]{0:T(512)} %cb_hbm.1, f32[768]{0:T(1024)} %tb_hbm.1, f32[192]{0:T(256)} %ub_hbm.1, bf16[3,3,3,384,384]{4,3,2,1,0:T(8,128)(2,1)} %cw_hbm.1, bf16[3,384,768]{2,1,0:T(8,128)(2,1)} %tw_hbm.1, ...), custom_call_target="tpu_custom_call" | custom-call | tf_op jit(solution)/shard_map/pallas_call | solution.py:502
  40.0 1.0 %copy.10 = bf16[2,4,320,192]{2,3,1,0:T(8,128)(2,1)} copy(bf16[2,4,320,192]{2,3,1,0:T(8,128)(2,1)S(1)} %bitcast.2) | data formatting | bytes 1966080

commit v9 on v8

--- a/solution.py
+++ b/solution.py
@@ -24,11 +24,11 @@
     frames, tiles,
     lat_hbm, gain_hbm, cb_hbm, tb_hbm, ub_hbm, cw_hbm, tw_hbm, uw_hbm,
     out_ref,
-    lat, act, act_hist, act_relay, parts, part_in, blk, blk_hist, blk_relay, dbl,
+    lat, act, act_hist, act_relay, parts, part_in, blk, blk_hist, dbl,
     gain_ref, cb_ref, tb_ref, ub_ref, cw, tw, uw, umat, acc, mixed, edge, wide_lo, wide_hi,
     lat_sem, bias_sem, cw_sem, tw_sem, uw_sem,
     a_send, a_recv, a_fsend, r_send, r_recv, b_send, b_recv, b_fsend,
-    p_down_sem, p_up_sem, b_down_sem, b_up_sem, d_up_sem, q_sem,
+    p_down_sem, p_up_sem, b_down_sem, b_up_sem, d_up_sem,
 ):
     rows, cols, chans = lat.shape
     outs_n = uw.shape[2]
@@ -187,14 +187,6 @@
             device_id={"tm": t + 2, "tile": partner}, device_id_type=MESH,
         )
 
-    blk_to_partner = pltpu.make_async_remote_copy(
-        blk.at[rows], blk_relay, q_sem.at[0], q_sem.at[1], device_id={"tile": partner}, device_id_type=MESH
-    )
-    blk_from_partner = pltpu.make_async_remote_copy(
-        blk_relay, blk_hist.at[0, rows], q_sem.at[2], b_recv.at[0, rows],
-        device_id={"tm": t + 2, "tile": partner}, device_id_type=MESH,
-    )
-
     order = tuple(range(rows))[::-1]
     lat_copy.wait()
     for copy in bias_copies:
@@ -352,20 +344,11 @@
     def _():
         blk_down.start()
 
-    @pl.when(relays)
-    def _():
-        blk_to_partner.start()
-
-    history_start(blk_copies, rows, direct)
+    history_start(blk_copies, rows)
     newest(rows)
 
     for r in range(rows):
         if r == last:
-            @pl.when(relays)
-            def _():
-                blk_to_partner.wait_recv()
-                blk_from_partner.start()
-
             @pl.when(has_up)
             def _():
                 blk_down.wait_recv()
@@ -460,15 +443,13 @@
 
     for r in range(rows):
         history_end(act_copies, r, has_next if r == order[0] else direct)
-        history_end(blk_copies, 1 + r, direct if r == last else has_next)
+        history_end(blk_copies, 1 + r)
 
     @pl.when(relays)
     def _():
         for r in order[1:]:
             to_partner(r).wait_send()
             from_partner(r).wait_send()
-        blk_to_partner.wait_send()
-        blk_from_partner.wait_send()
 
     @pl.when(has_up)
     def _():
@@ -513,7 +494,6 @@
             pltpu.VMEM((2,) + row, BF16),
             pltpu.VMEM((rows + 2,) + row, BF16),
             pltpu.VMEM((2, rows + 2) + row, BF16),
-            pltpu.VMEM(row, BF16),
             pltpu.VMEM((rows + 2, 2) + row, BF16),
             pltpu.VMEM((chans,), F32),
             pltpu.VMEM((chans,), F32),
@@ -532,7 +512,7 @@
             dma((2, rows)), dma((2, rows)), dma((rows,)),
             dma((2, rows)), dma((rows,)),
             dma((2, rows + 2)), dma((2, rows + 2)), dma((rows + 2,)),
-            dma((2,)), dma((2,)), dma((2,)), dma((2,)), dma((2,)), dma((3,)),
+            dma((2,)), dma((2,)), dma((2,)), dma((2,)), dma((2,)),
         ],
         compiler_params=pltpu.CompilerParams(
             collective_id=0, has_side_effects=True, vmem_limit_bytes=48 * 1024 * 1024

time: 41.1 us -> 34.8 us (0.85)
  the two profiles are of different devices: /device:TPU:6 before, /device:TPU:28 now
where the time goes in v9:
time: 34.8 us
  Pallas kernels  33.7 us (97%)
  local copies, waits for them, and re-layouts  1.02 us (3%)
    pallas_call x1, Pallas kernels, local(): pl.pallas_call(functools.partial(kernel, frames, tiles), out_shape=jax.Sh...  33.7 us
    unnamed x1, local copies, waits for them, and re-layouts  1.02 us

profile of v9, /device:TPU:28, one launch (start us, length us, event | category | flops | bytes accessed | tf_op | source)
XLA Modules:
  0.0 34.8 jit_solution(10779111419336436502)
XLA Ops:
  0.0 33.7 %shard_map.82 = bf16[2,4,192,320]{3,2,1,0:T(8,128)(2,1)S(1)} custom-call(bf16[1,2,160,384]{3,2,1,0:T(8,128)(2,1)} %lat_hbm.1, f32[384]{0:T(512)} %gain_hbm.1, f32[384]{0:T(512)} %cb_hbm.1, f32[768]{0:T(1024)} %tb_hbm.1, f32[192]{0:T(256)} %ub_hbm.1, bf16[3,3,3,384,384]{4,3,2,1,0:T(8,128)(2,1)} %cw_hbm.1, bf16[3,384,768]{2,1,0:T(8,128)(2,1)} %tw_hbm.1, ...), custom_call_target="tpu_custom_call" | custom-call | tf_op jit(solution)/shard_map/pallas_call | solution.py:483
  33.8 1.0 %copy.10 = bf16[2,4,320,192]{2,3,1,0:T(8,128)(2,1)} copy(bf16[2,4,320,192]{2,3,1,0:T(8,128)(2,1)S(1)} %bitcast.2) | data formatting | bytes 1966080

commit v10 on v9

--- a/solution.py
+++ b/solution.py
@@ -56,6 +56,28 @@
         copy = pltpu.make_async_copy(src, dst, bias_sem.at[k])
         copy.start()
         bias_copies.append(copy)
+    half = frames // 2
+    partner = s + 1 - 2 * lax.rem(s, 2)
+    relays = t // 2 == half // 2 - 1
+    relayed = t // 2 == half // 2
+    direct = jnp.logical_and(has_next, jnp.logical_not(relays))
+
+    sibling = t + 1 - 2 * lax.rem(t, 2)
+    barrier = pltpu.get_barrier_semaphore()
+
+    def greet(condition, where):
+        @pl.when(condition)
+        def _():
+            pl.semaphore_signal(barrier, inc=1, device_id=where, device_id_type=MESH)
+
+    pl.semaphore_signal(barrier, inc=1, device_id={"tm": sibling}, device_id_type=MESH)
+    greet(has_next, {"tm": t + 2})
+    greet(has_prev, {"tm": t - 2})
+    greet(relays, {"tm": t + 2, "tile": partner})
+    greet(relayed, {"tm": t - 2, "tile": partner})
+    greet(has_up, {"tile": s - 1})
+    greet(has_down, {"tile": s + 1})
+
     cw_copies = {}
     for dt in (2, 0, 1):
         for dh in range(3):
@@ -70,28 +92,6 @@
     tw_copy.start()
     uw_copy = pltpu.make_async_copy(uw_hbm, uw, uw_sem)
     uw_copy.start()
-
-    half = frames // 2
-    partner = s + 1 - 2 * lax.rem(s, 2)
-    relays = t // 2 == half // 2 - 1
-    relayed = t // 2 == half // 2
-    direct = jnp.logical_and(has_next, jnp.logical_not(relays))
-
-    sibling = t + 1 - 2 * lax.rem(t, 2)
-    barrier = pltpu.get_barrier_semaphore()
-
-    def greet(condition, where):
-        @pl.when(condition)
-        def _():
-            pl.semaphore_signal(barrier, inc=1, device_id=where, device_id_type=MESH)
-
-    pl.semaphore_signal(barrier, inc=1, device_id={"tm": sibling}, device_id_type=MESH)
-    greet(has_next, {"tm": t + 2})
-    greet(has_prev, {"tm": t - 2})
-    greet(relays, {"tm": t + 2, "tile": partner})
-    greet(relayed, {"tm": t - 2, "tile": partner})
-    greet(has_up, {"tile": s - 1})
-    greet(has_down, {"tile": s + 1})
 
     def history_copies(own, hist, send, recv, fsend):
         def nearer(r):
@@ -297,12 +297,13 @@
     def newest(j):
         mixed[j] = mix(blk[j], 2) + tb_ref[...].reshape(1, 2 * chans)
 
-    def mix_row(j):
+    def mix_far(j):
         @pl.when(has_prev)
         def _():
             history_far(blk_copies, j)
             mixed[j] += mix(blk_hist[0, j], 0)
 
+    def mix_near(j):
         @pl.when(has_near)
         def _():
             history_near(blk_copies, j)
@@ -310,6 +311,14 @@
 
         for f in range(2):
             dbl[j, f] = mixed[j, :, pl.ds(f * chans, chans)].astype(BF16)
+
+    def taps_dot(row, a, start, size):
+        return lax.dot_general(
+            row, umat[a, :, pl.ds(start, size)], (((1,), (1,)), ((), ())), preferred_element_type=F32
+        )
+
+    def stored_row(j):
+        return dbl[j].reshape(2 * cols, chans)
 
     @pl.when(has_up)
     def _():
@@ -354,7 +363,8 @@
                 blk_down.wait_recv()
                 history_start(blk_copies, 0)
 
-        mix_row(1 + r)
+        mix_far(1 + r)
+        mix_near(1 + r)
         if r == first:
             @pl.when(has_up & later)
             def _():
@@ -364,19 +374,13 @@
             def _():
                 blk_up.wait_recv()
                 blk_copies[0](rows + 1).start()
+
+            edge[0] = taps_dot(stored_row(1), 0, chans, chans)
 
     bias_row = ub_ref[...].reshape(1, outs_n)
     up_bias = jnp.concatenate(
         [bias_row[:, :low], bias_row[:, :low], bias_row[:, low:], bias_row[:, low:]], axis=1
     )
-
-    def taps_dot(row, a, start, size):
-        return lax.dot_general(
-            row, umat[a, :, pl.ds(start, size)], (((1,), (1,)), ((), ())), preferred_element_type=F32
-        )
-
-    def stored_row(j):
-        return dbl[j].reshape(2 * cols, chans)
 
     def upsample_row(a, r, result):
         center = result[:, : 2 * outs_n] + up_bias
@@ -404,16 +408,12 @@
                 both = jnp.concatenate([stored_row(r + a), stored_row(r + a + 1)], axis=1)
                 upsample_row(a, r, taps_dot(both, a, 0, 2 * chans))
 
-    edge[0] = taps_dot(stored_row(1), 0, chans, chans)
+    @pl.when(has_up)
+    def _():
+        newest(0)
+        mix_far(0)
+
     edge[1] = taps_dot(stored_row(rows), 1, 0, chans)
-
-    @pl.when(has_up)
-    def _():
-        newest(0)
-        mix_row(0)
-        edge[0] += taps_dot(stored_row(0), 0, 0, chans)
-
-    upsample_row(0, 0, edge[0])
 
     @pl.when(has_down & starts)
     def _():
@@ -440,6 +440,13 @@
         edge[1] += taps_dot(stored_row(rows + 1), 1, chans, chans)
 
     upsample_row(1, last, edge[1])
+
+    @pl.when(has_up)
+    def _():
+        mix_near(0)
+        edge[0] += taps_dot(stored_row(0), 0, 0, chans)
+
+    upsample_row(0, 0, edge[0])
 
     for r in range(rows):
         history_end(act_copies, r, has_next if r == order[0] else direct)

time: 34.8 us -> 35.8 us (1.029)
  the two profiles are of different devices: /device:TPU:28 before, /device:TPU:40 now
where the time goes in v10:
time: 35.8 us; the launch traced here: 35.7 us
  Pallas kernels  34.7 us (97%)
  local copies, waits for them, and re-layouts  1.02 us (3%)
    pallas_call x1, Pallas kernels, local(): pl.pallas_call(functools.partial(kernel, frames, tiles), out_shape=jax.Sh...  34.7 us
    unnamed x1, local copies, waits for them, and re-layouts  1.02 us

profile of v10, /device:TPU:40, one launch (start us, length us, event | category | flops | bytes accessed | tf_op | source)
XLA Modules:
  0.0 35.7 jit_solution(12785616232773280311)
XLA Ops:
  0.0 34.7 %shard_map.82 = bf16[2,4,192,320]{3,2,1,0:T(8,128)(2,1)S(1)} custom-call(bf16[1,2,160,384]{3,2,1,0:T(8,128)(2,1)} %lat_hbm.1, f32[384]{0:T(512)} %gain_hbm.1, f32[384]{0:T(512)} %cb_hbm.1, f32[768]{0:T(1024)} %tb_hbm.1, f32[192]{0:T(256)} %ub_hbm.1, bf16[3,3,3,384,384]{4,3,2,1,0:T(8,128)(2,1)} %cw_hbm.1, bf16[3,384,768]{2,1,0:T(8,128)(2,1)} %tw_hbm.1, ...), custom_call_target="tpu_custom_call" | custom-call | tf_op jit(solution)/shard_map/pallas_call | solution.py:490
  34.7 1.0 %copy.10 = bf16[2,4,320,192]{2,3,1,0:T(8,128)(2,1)} copy(bf16[2,4,320,192]{2,3,1,0:T(8,128)(2,1)S(1)} %bitcast.2) | data formatting | bytes 1966080

commit v11 on v10

--- a/solution.py
+++ b/solution.py
@@ -227,26 +227,31 @@
             to_partner(r).wait_recv()
             from_partner(r).start()
 
-    uw_copy.wait()
-    row_sets = {(0, 0): (0,), (0, 1): (1, 2), (1, 0): (0, 1), (1, 1): (2,)}
-    for (a, i), picks in row_sets.items():
-        taps = []
-        for kw in range(3):
-            tap = uw[picks[0], kw].astype(F32)
-            for kh in picks[1:]:
-                tap = tap + uw[kh, kw].astype(F32)
-            taps.append(tap)
-        center = (taps[1] + taps[2], taps[0] + taps[1])
-        sides = (taps[0], taps[2])
-        lanes = pl.ds(i * chans, chans)
-        for base, pair in ((0, center), (2 * outs_n, sides)):
-            for b in range(2):
-                value = pair[b].astype(BF16)
-                umat[a, pl.ds(base + b * low, low), lanes] = value[:low]
-                umat[a, pl.ds(base + 2 * low + b * high, high), lanes] = value[low:]
-
-    weights_ready(0)
-    weights_ready(1)
+    def sum_taps():
+        uw_copy.wait()
+        row_sets = {(0, 0): (0,), (0, 1): (1, 2), (1, 0): (0, 1), (1, 1): (2,)}
+        for (a, i), picks in row_sets.items():
+            taps = []
+            for kw in range(3):
+                tap = uw[picks[0], kw].astype(F32)
+                for kh in picks[1:]:
+                    tap = tap + uw[kh, kw].astype(F32)
+                taps.append(tap)
+            center = (taps[1] + taps[2], taps[0] + taps[1])
+            sides = (taps[0], taps[2])
+            lanes = pl.ds(i * chans, chans)
+            for base, pair in ((0, center), (2 * outs_n, sides)):
+                for b in range(2):
+                    value = pair[b].astype(BF16)
+                    umat[a, pl.ds(base + b * low, low), lanes] = value[:low]
+                    umat[a, pl.ds(base + 2 * low + b * high, high), lanes] = value[low:]
+
+    @pl.when(later)
+    def _():
+        sum_taps()
+        weights_ready(0)
+        weights_ready(1)
+
     for r in order:
         span = pl.ds(r * cols, cols)
         goes, stays = (0, chans) if r == last else (2 * chans, 0)
@@ -259,6 +264,11 @@
 
         @pl.when(has_near)
         def _():
+            if r == order[0]:
+                @pl.when(starts)
+                def _():
+                    weights_ready(1)
+
             history_near(act_copies, r)
             acc[span, pl.ds(goes, chans)] += conv(widen(act_hist[1, r]), 1, goes, chans)
 
@@ -354,6 +364,16 @@
         blk_down.start()
 
     history_start(blk_copies, rows)
+
+    @pl.when(starts)
+    def _():
+        sum_taps()
+        weights_ready(0)
+
+        @pl.when(t == 0)
+        def _():
+            weights_ready(1)
+
     newest(rows)
 
     for r in range(rows):

time: 35.8 us -> 33.4 us (0.933)
  the two profiles are of different devices: /device:TPU:40 before, /device:TPU:28 now
where the time goes in v11:
time: 33.4 us
  Pallas kernels  32.3 us (97%)
  local copies, waits for them, and re-layouts  1.02 us (3%)
    pallas_call x1, Pallas kernels, local(): pl.pallas_call(functools.partial(kernel, frames, tiles), out_shape=jax.Sh...  32.3 us
    unnamed x1, local copies, waits for them, and re-layouts  1.02 us

profile of v11, /device:TPU:28, one launch (start us, length us, event | category | flops | bytes accessed | tf_op | source)
XLA Modules:
  0.0 33.4 jit_solution(7818104710309853806)
XLA Ops:
  0.0 32.3 %shard_map.82 = bf16[2,4,192,320]{3,2,1,0:T(8,128)(2,1)S(1)} custom-call(bf16[1,2,160,384]{3,2,1,0:T(8,128)(2,1)} %lat_hbm.1, f32[384]{0:T(512)} %gain_hbm.1, f32[384]{0:T(512)} %cb_hbm.1, f32[768]{0:T(1024)} %tb_hbm.1, f32[192]{0:T(256)} %ub_hbm.1, bf16[3,3,3,384,384]{4,3,2,1,0:T(8,128)(2,1)} %cw_hbm.1, bf16[3,384,768]{2,1,0:T(8,128)(2,1)} %tw_hbm.1, ...), custom_call_target="tpu_custom_call" | custom-call | tf_op jit(solution)/shard_map/pallas_call | solution.py:510
  32.3 1.0 %copy.10 = bf16[2,4,320,192]{2,3,1,0:T(8,128)(2,1)} copy(bf16[2,4,320,192]{2,3,1,0:T(8,128)(2,1)S(1)} %bitcast.2) | data formatting | bytes 1966080

commit v12 on v11

--- a/solution.py
+++ b/solution.py
@@ -37,9 +37,11 @@
     cells = rows * cols
     t = lax.axis_index("tm")
     s = lax.axis_index("tile")
-    odd = lax.rem(t, 2) == 1
+    parity = lax.rem(t, 2)
+    odd = parity == 1
     even = jnp.logical_not(odd)
-    has_next = t + 2 < frames
+    following = t + 2 - parity
+    has_next = following < frames
     has_prev = t >= 2
     has_near = t >= 1
     starts = t < 2
@@ -59,7 +61,8 @@
     half = frames // 2
     partner = s + 1 - 2 * lax.rem(s, 2)
     relays = t // 2 == half // 2 - 1
-    relayed = t // 2 == half // 2
+    relayed = t == half
+    receives = jnp.logical_and(even, t >= 2)
     direct = jnp.logical_and(has_next, jnp.logical_not(relays))
 
     sibling = t + 1 - 2 * lax.rem(t, 2)
@@ -71,10 +74,12 @@
             pl.semaphore_signal(barrier, inc=1, device_id=where, device_id_type=MESH)
 
     pl.semaphore_signal(barrier, inc=1, device_id={"tm": sibling}, device_id_type=MESH)
-    greet(has_next, {"tm": t + 2})
-    greet(has_prev, {"tm": t - 2})
-    greet(relays, {"tm": t + 2, "tile": partner})
+    greet(has_next, {"tm": following})
+    greet(receives, {"tm": t - 2})
+    greet(receives, {"tm": t - 1})
+    greet(relays, {"tm": following, "tile": partner})
     greet(relayed, {"tm": t - 2, "tile": partner})
+    greet(relayed, {"tm": t - 1, "tile": partner})
     greet(has_up, {"tile": s - 1})
     greet(has_down, {"tile": s + 1})
 
@@ -102,13 +107,13 @@
 
         def farther(r):
             return pltpu.make_async_remote_copy(
-                own.at[r], hist.at[0, r], send.at[1, r], recv.at[0, r],
-                device_id={"tm": t + 2}, device_id_type=MESH,
+                own.at[r], hist.at[parity, r], send.at[1, r], recv.at[parity, r],
+                device_id={"tm": following}, device_id_type=MESH,
             )
 
         def forward(r):
             return pltpu.make_async_remote_copy(
-                hist.at[0, r], hist.at[1, r], fsend.at[r], recv.at[1, r],
+                hist.at[1, r], hist.at[0, r], fsend.at[r], recv.at[0, r],
                 device_id={"tm": sibling}, device_id_type=MESH,
             )
 
@@ -125,16 +130,16 @@
         def _():
             nearer(r).start()
 
+    def history_near(copies, r):
+        nearer, _, forward = copies
+        nearer(r).wait_recv()
+
+        @pl.when(receives)
+        def _():
+            forward(r).start()
+
     def history_far(copies, r):
-        _, farther, forward = copies
-        farther(r).wait_recv()
-
-        @pl.when(odd)
-        def _():
-            forward(r).start()
-
-    def history_near(copies, r):
-        copies[0](r).wait_recv()
+        copies[2](r).wait_recv()
 
     def history_end(copies, r, sends=has_next):
         nearer, farther, forward = copies
@@ -147,7 +152,7 @@
         def _():
             nearer(r).wait_send()
 
-        @pl.when(jnp.logical_and(odd, has_prev))
+        @pl.when(receives)
         def _():
             forward(r).wait_send()
 
@@ -172,7 +177,7 @@
         act[r] = (scaled * jax.nn.sigmoid(scaled)).astype(BF16)
 
     peers = 1
-    for condition in (has_next, has_prev, relays, relayed, has_up, has_down):
+    for condition in (has_next, receives, receives, relays, relayed, relayed, has_up, has_down):
         peers = peers + condition.astype(jnp.int32)
 
     def to_partner(r):
@@ -183,8 +188,8 @@
 
     def from_partner(r):
         return pltpu.make_async_remote_copy(
-            act_relay.at[r], act_hist.at[0, r], r_send.at[1, r], a_recv.at[0, r],
-            device_id={"tm": t + 2, "tile": partner}, device_id_type=MESH,
+            act_relay.at[r], act_hist.at[parity, r], r_send.at[1, r], a_recv.at[parity, r],
+            device_id={"tm": following, "tile": partner}, device_id_type=MESH,
         )
 
     order = tuple(range(rows))[::-1]
@@ -257,11 +262,6 @@
         goes, stays = (0, chans) if r == last else (2 * chans, 0)
         out_part = 1 if r == last else 0
 
-        @pl.when(has_prev)
-        def _():
-            history_far(act_copies, r)
-            acc[span, :] += conv(widen(act_hist[0, r]), 0, 0, 3 * chans)
-
         @pl.when(has_near)
         def _():
             if r == order[0]:
@@ -270,7 +270,12 @@
                     weights_ready(1)
 
             history_near(act_copies, r)
-            acc[span, pl.ds(goes, chans)] += conv(widen(act_hist[1, r]), 1, goes, chans)
+            acc[span, :] += conv(widen(act_hist[1, r]), 1, 0, 3 * chans)
+
+        @pl.when(has_prev)
+        def _():
+            history_far(act_copies, r)
+            acc[span, pl.ds(goes, chans)] += conv(widen(act_hist[0, r]), 0, goes, chans)
 
         parts[out_part] = acc[span, pl.ds(goes, chans)].astype(BF16)
         if r == last:
@@ -282,9 +287,9 @@
             def _():
                 part_up.start()
 
-        @pl.when(has_near)
-        def _():
-            acc[span, pl.ds(stays, 2 * chans)] += conv(widen(act_hist[1, r]), 1, stays, 2 * chans)
+        @pl.when(has_prev)
+        def _():
+            acc[span, pl.ds(stays, 2 * chans)] += conv(widen(act_hist[0, r]), 0, stays, 2 * chans)
 
     def finish_row(r):
         total = acc[pl.ds(r * cols, cols), pl.ds(chans, chans)]
@@ -307,17 +312,17 @@
     def newest(j):
         mixed[j] = mix(blk[j], 2) + tb_ref[...].reshape(1, 2 * chans)
 
+    def mix_near(j):
+        @pl.when(has_near)
+        def _():
+            history_near(blk_copies, j)
+            mixed[j] += mix(blk_hist[1, j], 1)
+
     def mix_far(j):
         @pl.when(has_prev)
         def _():
             history_far(blk_copies, j)
             mixed[j] += mix(blk_hist[0, j], 0)
-
-    def mix_near(j):
-        @pl.when(has_near)
-        def _():
-            history_near(blk_copies, j)
-            mixed[j] += mix(blk_hist[1, j], 1)
 
         for f in range(2):
             dbl[j, f] = mixed[j, :, pl.ds(f * chans, chans)].astype(BF16)
@@ -383,8 +388,8 @@
                 blk_down.wait_recv()
                 history_start(blk_copies, 0)
 
+        mix_near(1 + r)
         mix_far(1 + r)
-        mix_near(1 + r)
         if r == first:
             @pl.when(has_up & later)
             def _():
@@ -431,7 +436,7 @@
     @pl.when(has_up)
     def _():
         newest(0)
-        mix_far(0)
+        mix_near(0)
 
     edge[1] = taps_dot(stored_row(rows), 1, 0, chans)
 
@@ -463,7 +468,7 @@
 
     @pl.when(has_up)
     def _():
-        mix_near(0)
+        mix_far(0)
         edge[0] += taps_dot(stored_row(0), 0, 0, chans)
 
     upsample_row(0, 0, edge[0])

time: 33.4 us -> 34.7 us (1.039); the launches traced: 33.4 us -> 34.3 us
  Pallas kernels: 32.3 us -> 33.3 us
    pallas_call x1, Pallas kernels: 32.3 us -> 33.3 us  [local(): pl.pallas_call(functools.partial(kernel, frames, tiles), out_shape=jax.Sh...]
where the time goes in v12:
time: 34.7 us; the launch traced here: 34.3 us
  Pallas kernels  33.3 us (96%)
  local copies, waits for them, and re-layouts  1.02 us (3%)
    pallas_call x1, Pallas kernels, local(): pl.pallas_call(functools.partial(kernel, frames, tiles), out_shape=jax.Sh...  33.3 us
    unnamed x1, local copies, waits for them, and re-layouts  1.02 us

profile of v12, /device:TPU:28, one launch (start us, length us, event | category | flops | bytes accessed | tf_op | source)
XLA Modules:
  0.0 34.3 jit_solution(2116813137587026396)
XLA Ops:
  0.0 33.3 %shard_map.82 = bf16[2,4,192,320]{3,2,1,0:T(8,128)(2,1)S(1)} custom-call(bf16[1,2,160,384]{3,2,1,0:T(8,128)(2,1)} %lat_hbm.1, f32[384]{0:T(512)} %gain_hbm.1, f32[384]{0:T(512)} %cb_hbm.1, f32[768]{0:T(1024)} %tb_hbm.1, f32[192]{0:T(256)} %ub_hbm.1, bf16[3,3,3,384,384]{4,3,2,1,0:T(8,128)(2,1)} %cw_hbm.1, bf16[3,384,768]{2,1,0:T(8,128)(2,1)} %tw_hbm.1, ...), custom_call_target="tpu_custom_call" | custom-call | tf_op jit(solution)/shard_map/pallas_call | solution.py:515
  33.3 1.0 %copy.10 = bf16[2,4,320,192]{2,3,1,0:T(8,128)(2,1)} copy(bf16[2,4,320,192]{2,3,1,0:T(8,128)(2,1)S(1)} %bitcast.2) | data formatting | bytes 1966080

commit v13 on v11

--- a/solution.py
+++ b/solution.py
@@ -163,7 +163,7 @@
     part_up = to_tile(parts.at[0], part_in.at[1], p_up_sem, s - 1)
     blk_down = to_tile(blk.at[rows], blk.at[0], b_down_sem, s + 1)
     blk_up = to_tile(blk.at[1], blk.at[rows + 1], b_up_sem, s - 1)
-    dbl_up = to_tile(dbl.at[1], dbl.at[rows + 1], d_up_sem, s - 1)
+    dbl_up = [to_tile(dbl.at[1, f], dbl.at[rows + 1, f], d_up_sem.at[f], s - 1) for f in range(2)]
 
     def activate(r):
         values = lat[r].astype(F32)
@@ -189,8 +189,7 @@
 
     order = tuple(range(rows))[::-1]
     lat_copy.wait()
-    for copy in bias_copies:
-        copy.wait()
+    bias_copies[0].wait()
     for r in order:
         activate(r)
         if r == order[0]:
@@ -299,6 +298,8 @@
             total = total + part_in[1].astype(F32)
         blk[1 + r] = total.astype(BF16)
 
+    for copy in bias_copies[1:]:
+        copy.wait()
     tw_copy.wait()
 
     def mix(row, k):
@@ -388,7 +389,8 @@
         if r == first:
             @pl.when(has_up & later)
             def _():
-                dbl_up.start()
+                for copy in dbl_up:
+                    copy.start()
 
             @pl.when(has_down & (t == 0))
             def _():
@@ -402,7 +404,7 @@
         [bias_row[:, :low], bias_row[:, :low], bias_row[:, low:], bias_row[:, low:]], axis=1
     )
 
-    def upsample_row(a, r, result):
+    def upsample_row(a, r, result, which=(0, 1)):
         center = result[:, : 2 * outs_n] + up_bias
         sides = result[:, 2 * outs_n :]
         even = center[:, :low] + column_shift(sides[:, :low], cols, 1)
@@ -413,8 +415,8 @@
             lane < high, column_shift(tail, cols, 1), column_shift(tail, cols, -1)
         )
         swapped = pltpu.roll(tail, high, 1)
-        for f in range(2):
-            span = slice(f * cols, (f + 1) * cols)
+        for k, f in enumerate(which):
+            span = slice(k * cols, (k + 1) * cols)
             wide_lo[pl.ds(0, cols, stride=2), :] = even[span]
             wide_lo[pl.ds(1, cols, stride=2), :] = uneven[span]
             wide_hi[pl.ds(0, cols, stride=2), :] = tail[span]
@@ -435,6 +437,13 @@
 
     edge[1] = taps_dot(stored_row(rows), 1, 0, chans)
 
+    @pl.when(has_up)
+    def _():
+        mix_near(0)
+        edge[0] += taps_dot(stored_row(0), 0, 0, chans)
+
+    upsample_row(0, 0, edge[0])
+
     @pl.when(has_down & starts)
     def _():
         @pl.when(t == 1)
@@ -451,22 +460,18 @@
         for f in range(2):
             dbl[rows + 1, f] = mixed[rows + 1, :, pl.ds(f * chans, chans)].astype(BF16)
 
-    @pl.when(has_down & later)
-    def _():
-        dbl_up.wait_recv()
-
-    @pl.when(has_down)
-    def _():
-        edge[1] += taps_dot(stored_row(rows + 1), 1, chans, chans)
-
-    upsample_row(1, last, edge[1])
-
-    @pl.when(has_up)
-    def _():
-        mix_near(0)
-        edge[0] += taps_dot(stored_row(0), 0, 0, chans)
-
-    upsample_row(0, 0, edge[0])
+    for f in range(2):
+        frame = pl.ds(f * cols, cols)
+
+        @pl.when(has_down & later)
+        def _():
+            dbl_up[f].wait_recv()
+
+        @pl.when(has_down)
+        def _():
+            edge[1, frame] += taps_dot(dbl[rows + 1, f], 1, chans, chans)
+
+        upsample_row(1, last, edge[1, frame], (f,))
 
     for r in range(rows):
         history_end(act_copies, r, has_next if r == order[0] else direct)
@@ -485,7 +490,8 @@
 
         @pl.when(later)
         def _():
-            dbl_up.wait_send()
+            for copy in dbl_up:
+                copy.wait_send()
 
         @pl.when(starts)
         def _():
@@ -539,7 +545,7 @@
             dma((2, rows)), dma((2, rows)), dma((rows,)),
             dma((2, rows)), dma((rows,)),
             dma((2, rows + 2)), dma((2, rows + 2)), dma((rows + 2,)),
-            dma((2,)), dma((2,)), dma((2,)), dma((2,)), dma((2,)),
+            dma((2,)), dma((2,)), dma((2,)), dma((2,)), dma((2, 2)),
         ],
         compiler_params=pltpu.CompilerParams(
             collective_id=0, has_side_effects=True, vmem_limit_bytes=48 * 1024 * 1024

time: 33.4 us -> 33.8 us (1.012)
  Pallas kernels: 32.3 us -> 32.7 us
    pallas_call x1, Pallas kernels: 32.3 us -> 32.7 us  [local(): pl.pallas_call(functools.partial(kernel, frames, tiles), out_shape=jax.Sh...]
where the time goes in v13:
time: 33.8 us; the launch traced here: 33.7 us
  Pallas kernels  32.7 us (97%)
  local copies, waits for them, and re-layouts  1.02 us (3%)
    pallas_call x1, Pallas kernels, local(): pl.pallas_call(functools.partial(kernel, frames, tiles), out_shape=jax.Sh...  32.7 us
    unnamed x1, local copies, waits for them, and re-layouts  1.02 us

profile of v13, /device:TPU:28, one launch (start us, length us, event | category | flops | bytes accessed | tf_op | source)
XLA Modules:
  0.0 33.7 jit_solution(5332533865507268954)
XLA Ops:
  0.0 32.7 %shard_map.82 = bf16[2,4,192,320]{3,2,1,0:T(8,128)(2,1)S(1)} custom-call(bf16[1,2,160,384]{3,2,1,0:T(8,128)(2,1)} %lat_hbm.1, f32[384]{0:T(512)} %gain_hbm.1, f32[384]{0:T(512)} %cb_hbm.1, f32[768]{0:T(1024)} %tb_hbm.1, f32[192]{0:T(256)} %ub_hbm.1, bf16[3,3,3,384,384]{4,3,2,1,0:T(8,128)(2,1)} %cw_hbm.1, bf16[3,384,768]{2,1,0:T(8,128)(2,1)} %tw_hbm.1, ...), custom_call_target="tpu_custom_call" | custom-call | tf_op jit(solution)/shard_map/pallas_call | solution.py:516
  32.7 1.0 %copy.10 = bf16[2,4,320,192]{2,3,1,0:T(8,128)(2,1)} copy(bf16[2,4,320,192]{2,3,1,0:T(8,128)(2,1)S(1)} %bitcast.2) | data formatting | bytes 1966080

commit v14 on v13

--- a/solution.py
+++ b/solution.py
@@ -437,41 +437,41 @@
 
     edge[1] = taps_dot(stored_row(rows), 1, 0, chans)
 
+    @pl.when(has_down & starts)
+    def _():
+        @pl.when(t == 1)
+        def _():
+            blk_up.wait_recv()
+
+        newest(rows + 1)
+
+        @pl.when(t == 1)
+        def _():
+            history_near(blk_copies, rows + 1)
+            mixed[rows + 1] += mix(blk_hist[1, rows + 1], 1)
+
+        for f in range(2):
+            dbl[rows + 1, f] = mixed[rows + 1, :, pl.ds(f * chans, chans)].astype(BF16)
+
+    for f in range(2):
+        frame = pl.ds(f * cols, cols)
+
+        @pl.when(has_down & later)
+        def _():
+            dbl_up[f].wait_recv()
+
+        @pl.when(has_down)
+        def _():
+            edge[1, frame] += taps_dot(dbl[rows + 1, f], 1, chans, chans)
+
+        upsample_row(1, last, edge[1, frame], (f,))
+
     @pl.when(has_up)
     def _():
         mix_near(0)
         edge[0] += taps_dot(stored_row(0), 0, 0, chans)
 
     upsample_row(0, 0, edge[0])
-
-    @pl.when(has_down & starts)
-    def _():
-        @pl.when(t == 1)
-        def _():
-            blk_up.wait_recv()
-
-        newest(rows + 1)
-
-        @pl.when(t == 1)
-        def _():
-            history_near(blk_copies, rows + 1)
-            mixed[rows + 1] += mix(blk_hist[1, rows + 1], 1)
-
-        for f in range(2):
-            dbl[rows + 1, f] = mixed[rows + 1, :, pl.ds(f * chans, chans)].astype(BF16)
-
-    for f in range(2):
-        frame = pl.ds(f * cols, cols)
-
-        @pl.when(has_down & later)
-        def _():
-            dbl_up[f].wait_recv()
-
-        @pl.when(has_down)
-        def _():
-            edge[1, frame] += taps_dot(dbl[rows + 1, f], 1, chans, chans)
-
-        upsample_row(1, last, edge[1, frame], (f,))
 
     for r in range(rows):
         history_end(act_copies, r, has_next if r == order[0] else direct)

time: 33.8 us -> 33.8 us (level)
  no operation moved by 1% of the time
where the time goes in v14:
time: 33.8 us; the launch traced here: 33.7 us
  Pallas kernels  32.7 us (97%)
  local copies, waits for them, and re-layouts  1.02 us (3%)
    pallas_call x1, Pallas kernels, local(): pl.pallas_call(functools.partial(kernel, frames, tiles), out_shape=jax.Sh...  32.7 us
    unnamed x1, local copies, waits for them, and re-layouts  1.02 us

profile of v14, /device:TPU:28, one launch (start us, length us, event | category | flops | bytes accessed | tf_op | source)
XLA Modules:
  0.0 33.7 jit_solution(15295223447123841163)
XLA Ops:
  0.0 32.7 %shard_map.82 = bf16[2,4,192,320]{3,2,1,0:T(8,128)(2,1)S(1)} custom-call(bf16[1,2,160,384]{3,2,1,0:T(8,128)(2,1)} %lat_hbm.1, f32[384]{0:T(512)} %gain_hbm.1, f32[384]{0:T(512)} %cb_hbm.1, f32[768]{0:T(1024)} %tb_hbm.1, f32[192]{0:T(256)} %ub_hbm.1, bf16[3,3,3,384,384]{4,3,2,1,0:T(8,128)(2,1)} %cw_hbm.1, bf16[3,384,768]{2,1,0:T(8,128)(2,1)} %tw_hbm.1, ...), custom_call_target="tpu_custom_call" | custom-call | tf_op jit(solution)/shard_map/pallas_call | solution.py:516
  32.7 1.0 %copy.10 = bf16[2,4,320,192]{2,3,1,0:T(8,128)(2,1)} copy(bf16[2,4,320,192]{2,3,1,0:T(8,128)(2,1)S(1)} %bitcast.2) | data formatting | bytes 1966080

commit v15 on v11

--- a/solution.py
+++ b/solution.py
@@ -189,8 +189,7 @@
 
     order = tuple(range(rows))[::-1]
     lat_copy.wait()
-    for copy in bias_copies:
-        copy.wait()
+    bias_copies[0].wait()
     for r in order:
         activate(r)
         if r == order[0]:
@@ -299,6 +298,8 @@
             total = total + part_in[1].astype(F32)
         blk[1 + r] = total.astype(BF16)
 
+    for copy in bias_copies[1:]:
+        copy.wait()
     tw_copy.wait()
 
     def mix(row, k):
@@ -383,6 +384,8 @@
                 blk_down.wait_recv()
                 history_start(blk_copies, 0)
 
+            edge[0] = taps_dot(stored_row(1), 0, chans, chans)
+
         mix_far(1 + r)
         mix_near(1 + r)
         if r == first:
@@ -394,8 +397,6 @@
             def _():
                 blk_up.wait_recv()
                 blk_copies[0](rows + 1).start()
-
-            edge[0] = taps_dot(stored_row(1), 0, chans, chans)
 
     bias_row = ub_ref[...].reshape(1, outs_n)
     up_bias = jnp.concatenate(

time: 33.4 us -> 33.4 us (level)
  no operation moved by 1% of the time
where the time goes in v15:
time: 33.4 us
  Pallas kernels  32.3 us (97%)
  local copies, waits for them, and re-layouts  1.02 us (3%)
    pallas_call x1, Pallas kernels, local(): pl.pallas_call(functools.partial(kernel, frames, tiles), out_shape=jax.Sh...  32.3 us
    unnamed x1, local copies, waits for them, and re-layouts  1.02 us

profile of v15, /device:TPU:28, one launch (start us, length us, event | category | flops | bytes accessed | tf_op | source)
XLA Modules:
  0.0 33.4 jit_solution(9126235820188230413)
XLA Ops:
  0.0 32.3 %shard_map.82 = bf16[2,4,192,320]{3,2,1,0:T(8,128)(2,1)S(1)} custom-call(bf16[1,2,160,384]{3,2,1,0:T(8,128)(2,1)} %lat_hbm.1, f32[384]{0:T(512)} %gain_hbm.1, f32[384]{0:T(512)} %cb_hbm.1, f32[768]{0:T(1024)} %tb_hbm.1, f32[192]{0:T(256)} %ub_hbm.1, bf16[3,3,3,384,384]{4,3,2,1,0:T(8,128)(2,1)} %cw_hbm.1, bf16[3,384,768]{2,1,0:T(8,128)(2,1)} %tw_hbm.1, ...), custom_call_target="tpu_custom_call" | custom-call | tf_op jit(solution)/shard_map/pallas_call | solution.py:511
  32.3 1.0 %copy.10 = bf16[2,4,320,192]{2,3,1,0:T(8,128)(2,1)} copy(bf16[2,4,320,192]{2,3,1,0:T(8,128)(2,1)S(1)} %bitcast.2) | data formatting | bytes 1966080

commit v16 on v11

--- a/solution.py
+++ b/solution.py
@@ -49,6 +49,28 @@
 
     lat_copy = pltpu.make_async_copy(lat_hbm.at[0], lat, lat_sem)
     lat_copy.start()
+    half = frames // 2
+    partner = s + 1 - 2 * lax.rem(s, 2)
+    relays = t // 2 == half // 2 - 1
+    relayed = t // 2 == half // 2
+    direct = jnp.logical_and(has_next, jnp.logical_not(relays))
+
+    sibling = t + 1 - 2 * lax.rem(t, 2)
+    barrier = pltpu.get_barrier_semaphore()
+
+    def greet(condition, where):
+        @pl.when(condition)
+        def _():
+            pl.semaphore_signal(barrier, inc=1, device_id=where, device_id_type=MESH)
+
+    pl.semaphore_signal(barrier, inc=1, device_id={"tm": sibling}, device_id_type=MESH)
+    greet(has_next, {"tm": t + 2})
+    greet(has_prev, {"tm": t - 2})
+    greet(relays, {"tm": t + 2, "tile": partner})
+    greet(relayed, {"tm": t - 2, "tile": partner})
+    greet(has_up, {"tile": s - 1})
+    greet(has_down, {"tile": s + 1})
+
     bias_copies = []
     for k, (src, dst) in enumerate(
         ((gain_hbm, gain_ref), (cb_hbm, cb_ref), (tb_hbm, tb_ref), (ub_hbm, ub_ref))
@@ -56,27 +78,6 @@
         copy = pltpu.make_async_copy(src, dst, bias_sem.at[k])
         copy.start()
         bias_copies.append(copy)
-    half = frames // 2
-    partner = s + 1 - 2 * lax.rem(s, 2)
-    relays = t // 2 == half // 2 - 1
-    relayed = t // 2 == half // 2
-    direct = jnp.logical_and(has_next, jnp.logical_not(relays))
-
-    sibling = t + 1 - 2 * lax.rem(t, 2)
-    barrier = pltpu.get_barrier_semaphore()
-
-    def greet(condition, where):
-        @pl.when(condition)
-        def _():
-            pl.semaphore_signal(barrier, inc=1, device_id=where, device_id_type=MESH)
-
-    pl.semaphore_signal(barrier, inc=1, device_id={"tm": sibling}, device_id_type=MESH)
-    greet(has_next, {"tm": t + 2})
-    greet(has_prev, {"tm": t - 2})
-    greet(relays, {"tm": t + 2, "tile": partner})
-    greet(relayed, {"tm": t - 2, "tile": partner})
-    greet(has_up, {"tile": s - 1})
-    greet(has_down, {"tile": s + 1})
 
     cw_copies = {}
     for dt in (2, 0, 1):

time: 33.4 us -> 35.1 us (1.051)
  Pallas kernels: 32.3 us -> 34 us
    pallas_call x1, Pallas kernels: 32.3 us -> 34 us  [local(): pl.pallas_call(functools.partial(kernel, frames, tiles), out_shape=jax.Sh...]
where the time goes in v16:
time: 35.1 us; the launch traced here: 35 us
  Pallas kernels  34 us (97%)
  local copies, waits for them, and re-layouts  1.02 us (3%)
    pallas_call x1, Pallas kernels, local(): pl.pallas_call(functools.partial(kernel, frames, tiles), out_shape=jax.Sh...  34 us
    unnamed x1, local copies, waits for them, and re-layouts  1.02 us

profile of v16, /device:TPU:28, one launch (start us, length us, event | category | flops | bytes accessed | tf_op | source)
XLA Modules:
  0.0 35.0 jit_solution(17132266085335717461)
XLA Ops:
  0.0 34.0 %shard_map.82 = bf16[2,4,192,320]{3,2,1,0:T(8,128)(2,1)S(1)} custom-call(bf16[1,2,160,384]{3,2,1,0:T(8,128)(2,1)} %lat_hbm.1, f32[384]{0:T(512)} %gain_hbm.1, f32[384]{0:T(512)} %cb_hbm.1, f32[768]{0:T(1024)} %tb_hbm.1, f32[192]{0:T(256)} %ub_hbm.1, bf16[3,3,3,384,384]{4,3,2,1,0:T(8,128)(2,1)} %cw_hbm.1, bf16[3,384,768]{2,1,0:T(8,128)(2,1)} %tw_hbm.1, ...), custom_call_target="tpu_custom_call" | custom-call | tf_op jit(solution)/shard_map/pallas_call | solution.py:511
  34.0 1.0 %copy.10 = bf16[2,4,320,192]{2,3,1,0:T(8,128)(2,1)} copy(bf16[2,4,320,192]{2,3,1,0:T(8,128)(2,1)S(1)} %bitcast.2) | data formatting | bytes 1966080
